TPU v7x, 32 devices: a whole 2x2x4 slice. The times are simulated.
32 devices in a mesh: branch: 2 (over x), dp: 16 (over z, y, core).
Axes of the slice: x: 2, y: 2, z: 4, core: 2. Of those that a mesh axis runs over, the one named last changes fastest.
Arguments:
- inputs: bfloat16 [32, 1024, 768], P('dp'), may hold values from -6 to 6
- segments: int32 [32, 1024], P('dp'), may hold values from 0 to 7, never falling along the last dimension, each value on 1 to 512 neighbouring positions
- query_weight: bfloat16 [768, 384], replicated, may hold values from -0.21875 to 0.21875
- query_bias: float32 [384], replicated, may hold values from -1 to 1
- branch_weights: bfloat16 [2, 2, 768, 384], P('branch'), may hold values from -0.21875 to 0.21875
- value_bias: float32 [384], replicated, may hold values from -1 to 1
- depthwise: float32 [9, 768], replicated, may hold values from -2 to 2
- point_bias: float32 [384], replicated, may hold values from -1 to 1
- kernel_weight: bfloat16 [384, 54], replicated, may hold values from -0.3125 to 0.3125
- kernel_bias: float32 [54], replicated, may hold values from -2 to 2
- conv_bias: float32 [384], replicated, may hold values from -1 to 1
- output_weight: bfloat16 [768, 768], replicated, may hold values from -0.875 to 0.875
- output_bias: float32 [768], replicated, may hold values from -1 to 1
- first_gain: float32 [768], replicated, may hold values from 0.5 to 1.5
- first_shift: float32 [768], replicated, may hold values from -1 to 1
- up_weight: bfloat16 [2, 384, 1536], replicated, may hold values from -0.3125 to 0.3125
- up_bias: float32 [2, 1536], replicated, may hold values from -1 to 1
- down_weight: bfloat16 [2, 1536, 384], replicated, may hold values from -0.15625 to 0.15625
- down_bias: float32 [2, 384], replicated, may hold values from -1 to 1
- second_gain: float32 [768], replicated, may hold values from 0.5 to 1.5
- second_shift: float32 [768], replicated, may hold values from -1 to 1
- cotangent: bfloat16 [32, 1024, 768], P('dp', 'branch'), may hold values from -6 to 6
Outputs:
- activations: bfloat16 [32, 1024, 768], P('dp', 'branch')
- input_grad: float32 [32, 1024, 768], P('dp', 'branch')
- query_weight_grad: float32 [768, 384], replicated
- query_bias_grad: float32 [384], replicated
- branch_weights_grad: float32 [2, 2, 768, 384], P('branch')
- value_bias_grad: float32 [384], replicated
- depthwise_kernel_gradient: float32 [9, 768], replicated
- point_bias_grad: float32 [384], replicated
- kernel_weight_grad: float32 [384, 54], replicated
- kernel_bias_grad: float32 [54], replicated
- conv_bias_grad: float32 [384], replicated
- output_weight_grad: float32 [768, 768], replicated
- output_bias_grad: float32 [768], replicated
- first_gain_grad: float32 [768], replicated
- first_shift_grad: float32 [768], replicated
- up_weight_grad: float32 [2, 384, 1536], replicated
- up_bias_grad: float32 [2, 1536], replicated
- down_weight_grad: float32 [2, 1536, 384], replicated
- down_bias_grad: float32 [2, 384], replicated
- second_gain_grad: float32 [768], replicated
- second_shift_grad: float32 [768], replicated
Inputs may be any that keep to these rules, and one draw needn't show every extreme that they name: `segments`: in each sequence the document ids never fall, every document holds 1 to half of 1024 tokens, and some document holds exactly half of 1024.
All inputs are finite; a program needn't handle non-finite values.
Results may differ from a plain program's by a relative error of at most 0.02.
Values may be sent and summed in bfloat16 or wider, within the bound.
No kernel may reach another device: no remote copies, remote signals or barrier semaphores. Data moves between devices by JAX's collectives and lax.ppermute only.
A program may use at most 256 MiB of HBM per device.

v0:
```python
import jax
import jax.numpy as jnp
from jax import lax
from jax.sharding import PartitionSpec as P

HEADS = 6
HEAD = 64
KERNEL = 9
GROUPS = 2


EPS = 1e-12
BIG = -1e30


def shortened(shard):
    return jax.tree.map(lambda a: a.astype(jnp.bfloat16) if a.dtype == jnp.float32 else a, shard)


def matmul(left_operand, right_operand):
    return jnp.einsum(
        "vzt,ta->vza", left_operand, right_operand, preferred_element_type=jnp.float32
    )


def matmul_back(left_operand, right_operand):
    return jnp.einsum(
        "ozj,nj->ozn", left_operand, right_operand, preferred_element_type=jnp.float32
    )


def outer_sum(left_operand, right_operand):
    return jnp.einsum(
        "oer,oeu->ru", left_operand, right_operand, preferred_element_type=jnp.float32
    )


def shifted(array_in, offset):
    half_window = KERNEL // 2
    widths = [(0, 0)] * array_in.ndim
    widths[1] = (half_window, half_window)
    padded = jnp.pad(array_in, widths)
    return lax.slice_in_dim(
        padded, half_window + offset, half_window + offset + array_in.shape[1], axis=1
    )


def window_masks(segments):
    half_window = KERNEL // 2
    padded = jnp.pad(segments, ((0, 0), (half_window, half_window)), constant_values=-1)
    tap_masks = []
    for tap_index in range(KERNEL):
        shifted_ids = lax.slice_in_dim(padded, tap_index, tap_index + segments.shape[1], axis=1)
        tap_masks.append((shifted_ids == segments).astype(jnp.float32))
    return tap_masks


def norm_apply_forward(residual, norm_gain, norm_shift):
    center = residual - jnp.mean(residual, axis=-1, keepdims=True)
    inverse = lax.rsqrt(jnp.mean(center * center, axis=-1, keepdims=True) + EPS)
    normed = center * inverse
    return (normed * norm_gain + norm_shift, normed, inverse)


def norm_backward(grad_out, normed, inverse, norm_gain):
    scaled = grad_out * norm_gain
    return inverse * (
        scaled
        - jnp.mean(scaled, axis=-1, keepdims=True)
        - normed * jnp.mean(scaled * normed, axis=-1, keepdims=True)
    )


def gelu_exact(values):
    return jax.nn.gelu(values, approximate=False)


def blocked_rows(array_in, row_block):
    seq_count, length = (array_in.shape[0], array_in.shape[1])
    shaped = array_in.reshape((seq_count, length // row_block, row_block) + array_in.shape[2:])
    order = (1, 0) + tuple(range(2, shaped.ndim))
    return shaped.transpose(order)


def attention_scores(query_block, seg_block, key_heads, segments):
    scores = jnp.einsum(
        "sqhe,skhe->shqk", query_block, key_heads, preferred_element_type=jnp.float32
    ) * HEAD ** (-0.5)
    same_doc = seg_block[:, None, :, None] == segments[:, None, None, :]
    return jnp.where(same_doc, scores, BIG)


def attention_forward(queries, key_rows, value_rows, segments):
    seq_count, length = (queries.shape[0], queries.shape[1])
    row_block = min(512, length)
    query_heads = blocked_rows(queries.reshape(seq_count, length, HEADS, HEAD), row_block)
    seg_blocks = blocked_rows(segments, row_block)
    key_heads = key_rows.reshape(seq_count, length, HEADS, HEAD)
    value_heads = value_rows.reshape(seq_count, length, HEADS, HEAD)

    def one_block(pieces):
        query_block, seg_block = pieces
        scores = attention_scores(query_block, seg_block, key_heads, segments)
        row_peak = jnp.max(scores, axis=-1, keepdims=True)
        powers = jnp.exp(scores - row_peak)
        summed = jnp.sum(powers, axis=-1, keepdims=True)
        weights = (powers / summed).astype(jnp.bfloat16)
        outputs = jnp.einsum(
            "shqk,skhe->sqhe", weights, value_heads, preferred_element_type=jnp.float32
        )
        return (outputs.astype(jnp.bfloat16), (row_peak + jnp.log(summed))[..., 0])

    outputs, log_totals = lax.map(one_block, (query_heads, seg_blocks))
    return (outputs.transpose(1, 0, 2, 3, 4).reshape(seq_count, length, HEADS * HEAD), log_totals)


def attention_backward(
    inputs, queries, key_rows, value_rows, segments, log_totals, grad_out, own_weights
):
    seq_count, length = (queries.shape[0], queries.shape[1])
    row_block = min(512, length)
    score_scale = HEAD ** (-0.5)
    query_heads = blocked_rows(queries.reshape(seq_count, length, HEADS, HEAD), row_block)
    grad_heads = blocked_rows(grad_out.reshape(seq_count, length, HEADS, HEAD), row_block)
    seg_blocks = blocked_rows(segments, row_block)
    key_heads = key_rows.reshape(seq_count, length, HEADS, HEAD)
    value_heads = value_rows.reshape(seq_count, length, HEADS, HEAD)

    def one_block(carried, pieces):
        key_grad, value_grad = carried
        query_block, seg_block, grad_block, block_totals = pieces
        scores = attention_scores(query_block, seg_block, key_heads, segments)
        row_probs = jnp.exp(scores - block_totals[..., None])
        value_grad = value_grad + jnp.einsum(
            "shqk,sqhe->skhe",
            row_probs.astype(jnp.bfloat16),
            grad_block,
            preferred_element_type=jnp.float32,
        )
        prob_grad = jnp.einsum(
            "sqhe,skhe->shqk", grad_block, value_heads, preferred_element_type=jnp.float32
        )
        score_grad = (
            row_probs * (prob_grad - jnp.sum(row_probs * prob_grad, axis=-1, keepdims=True))
        ).astype(jnp.bfloat16)
        query_grad = (
            jnp.einsum("shqk,skhe->sqhe", score_grad, key_heads, preferred_element_type=jnp.float32)
            * score_scale
        )
        key_grad = key_grad + jnp.einsum(
            "shqk,sqhe->skhe", score_grad, query_block, preferred_element_type=jnp.float32
        )
        return ((key_grad, value_grad), query_grad)

    empty_grad = jnp.zeros((seq_count, length, HEADS, HEAD), jnp.float32)
    (key_grad, value_grad), query_grads = lax.scan(
        one_block, (empty_grad, empty_grad), (query_heads, seg_blocks, grad_heads, log_totals)
    )
    query_part = query_grads.transpose(1, 0, 2, 3, 4).reshape(seq_count, length, HEADS * HEAD)
    key_low = (key_grad * score_scale).reshape(seq_count, length, HEADS * HEAD).astype(jnp.bfloat16)
    value_low = value_grad.reshape(seq_count, length, HEADS * HEAD).astype(jnp.bfloat16)
    stack_grad = jnp.stack([outer_sum(inputs, key_low), outer_sum(inputs, value_low)])
    input_slice = matmul_back(key_low, own_weights[0]) + matmul_back(value_low, own_weights[1])
    value_bias_grad = jnp.sum(value_low.astype(jnp.float32), axis=(0, 1))
    return (query_part, input_slice, stack_grad, value_bias_grad)


def conv_pieces(
    inputs,
    inputs_f,
    queries,
    segments,
    own_weights,
    depthwise,
    point_bias,
    kernel_weight,
    kernel_bias,
    conv_bias,
):
    tap_masks = window_masks(segments)
    half_window = KERNEL // 2
    seq_count, length = (queries.shape[0], queries.shape[1])
    depth_out = jnp.zeros(inputs_f.shape, jnp.float32)
    for tap_index in range(KERNEL):
        depth_out = (
            depth_out
            + depthwise[tap_index]
            * shifted(inputs_f, tap_index - half_window)
            * tap_masks[tap_index][..., None]
        )
    depth_low = depth_out.astype(jnp.bfloat16)
    key_conv = (matmul(depth_low, own_weights[0]) + point_bias).astype(jnp.bfloat16)
    mixing = (key_conv.astype(jnp.float32) * queries.astype(jnp.float32)).astype(jnp.bfloat16)
    logits = (matmul(mixing, kernel_weight) + kernel_bias).reshape(seq_count, length, HEADS, KERNEL)
    tap_probs = jax.nn.softmax(logits, axis=-1)
    conv_values = (
        (matmul(inputs, own_weights[1]) + conv_bias)
        .astype(jnp.bfloat16)
        .reshape(seq_count, length, HEADS, HEAD)
    )
    return (tap_masks, depth_low, key_conv, mixing, tap_probs, conv_values)


def conv_forward(
    inputs,
    inputs_f,
    queries,
    segments,
    own_weights,
    depthwise,
    point_bias,
    kernel_weight,
    kernel_bias,
    conv_bias,
):
    tap_masks, depth_low, key_conv, mixing, tap_probs, conv_values = conv_pieces(
        inputs,
        inputs_f,
        queries,
        segments,
        own_weights,
        depthwise,
        point_bias,
        kernel_weight,
        kernel_bias,
        conv_bias,
    )
    half_window = KERNEL // 2
    seq_count, length = (queries.shape[0], queries.shape[1])
    tap_low = tap_probs.astype(jnp.bfloat16).astype(jnp.float32)
    values_f = conv_values.astype(jnp.float32)
    mixed = jnp.zeros(values_f.shape, jnp.float32)
    for tap_index in range(KERNEL):
        mixed = (
            mixed
            + tap_low[..., tap_index : tap_index + 1]
            * shifted(values_f, tap_index - half_window)
            * tap_masks[tap_index][..., None, None]
        )
    return mixed.reshape(seq_count, length, HEADS * HEAD).astype(jnp.bfloat16)


def conv_backward(
    inputs,
    inputs_f,
    queries,
    segments,
    own_weights,
    depthwise,
    point_bias,
    kernel_weight,
    kernel_bias,
    conv_bias,
    grad_out,
):
    tap_masks, depth_low, key_conv, mixing, tap_probs, conv_values = conv_pieces(
        inputs,
        inputs_f,
        queries,
        segments,
        own_weights,
        depthwise,
        point_bias,
        kernel_weight,
        kernel_bias,
        conv_bias,
    )
    half_window = KERNEL // 2
    seq_count, length = (queries.shape[0], queries.shape[1])
    grad_mixed = grad_out.astype(jnp.float32).reshape(seq_count, length, HEADS, HEAD)
    values_f = conv_values.astype(jnp.float32)
    tap_low = tap_probs.astype(jnp.bfloat16).astype(jnp.float32)
    tap_grads = []
    values_grad = jnp.zeros(values_f.shape, jnp.float32)
    for tap_index in range(KERNEL):
        offset = tap_index - half_window
        mask_now = tap_masks[tap_index][..., None, None]
        tap_grads.append(jnp.sum(grad_mixed * shifted(values_f, offset) * mask_now, axis=-1))
        values_grad = values_grad + shifted(
            tap_low[..., tap_index : tap_index + 1] * grad_mixed * mask_now, -offset
        )
    tap_grad = jnp.stack(tap_grads, axis=-1)
    logit_grad = tap_probs * (tap_grad - jnp.sum(tap_probs * tap_grad, axis=-1, keepdims=True))
    logit_grad = logit_grad.astype(jnp.bfloat16).reshape(seq_count, length, HEADS * KERNEL)
    kernel_bias_grad = jnp.sum(logit_grad.astype(jnp.float32), axis=(0, 1))
    kernel_weight_grad = outer_sum(mixing, logit_grad)
    mixing_grad = matmul_back(logit_grad, kernel_weight)
    key_conv_grad = (mixing_grad * queries.astype(jnp.float32)).astype(jnp.bfloat16)
    query_part = mixing_grad * key_conv.astype(jnp.float32)
    point_bias_grad = jnp.sum(key_conv_grad.astype(jnp.float32), axis=(0, 1))
    depth_grad = matmul_back(key_conv_grad, own_weights[0])
    tap_row_values = []
    input_slice = jnp.zeros(inputs_f.shape, jnp.float32)
    for tap_index in range(KERNEL):
        offset = tap_index - half_window
        masked = depth_grad * tap_masks[tap_index][..., None]
        tap_row_values.append(jnp.sum(masked * shifted(inputs_f, offset), axis=(0, 1)))
        input_slice = input_slice + shifted(masked * depthwise[tap_index], -offset)
    depthwise_kernel_gradient = jnp.stack(tap_row_values)
    values_low = values_grad.reshape(seq_count, length, HEADS * HEAD).astype(jnp.bfloat16)
    conv_bias_grad = jnp.sum(values_low.astype(jnp.float32), axis=(0, 1))
    input_slice = input_slice + matmul_back(values_low, own_weights[1])
    stack_grad = jnp.stack([outer_sum(depth_low, key_conv_grad), outer_sum(inputs, values_low)])
    return (
        query_part,
        input_slice,
        stack_grad,
        depthwise_kernel_gradient,
        point_bias_grad,
        kernel_weight_grad,
        kernel_bias_grad,
        conv_bias_grad,
    )


def local(
    inputs,
    segments,
    query_weight,
    query_bias,
    branch_weights,
    value_bias,
    depthwise,
    point_bias,
    kernel_weight,
    kernel_bias,
    conv_bias,
    output_weight,
    output_bias,
    first_gain,
    first_shift,
    up_weight,
    up_bias,
    down_weight,
    down_bias,
    second_gain,
    second_shift,
    cotangent,
):
    seq_count, length, features = inputs.shape
    half_len = length // 2
    branch_side = lax.axis_index("branch")
    own_weights = branch_weights[0]
    inputs_f = inputs.astype(jnp.float32)
    queries = (matmul(inputs, query_weight) + query_bias).astype(jnp.bfloat16)
    row_block = min(512, length)

    def attention_side(unused_in):
        key_rows = matmul(inputs, own_weights[0]).astype(jnp.bfloat16)
        value_rows = (matmul(inputs, own_weights[1]) + value_bias).astype(jnp.bfloat16)
        return attention_forward(queries, key_rows, value_rows, segments)

    def conv_side(unused_in):
        mixed = conv_forward(
            inputs,
            inputs_f,
            queries,
            segments,
            own_weights,
            depthwise,
            point_bias,
            kernel_weight,
            kernel_bias,
            conv_bias,
        )
        empty_totals = jnp.zeros((length // row_block, seq_count, HEADS, row_block), jnp.float32)
        return (mixed, empty_totals)

    branch_out, log_totals = lax.cond(branch_side == 0, attention_side, conv_side, inputs)
    joined_parts = lax.all_to_all(branch_out, "branch", split_axis=1, concat_axis=2, tiled=True)
    own_rows = lax.dynamic_slice_in_dim(inputs, branch_side * half_len, half_len, 1)
    hidden = matmul(joined_parts, output_weight) + output_bias
    normed_one_out, normed_one, inverse_one = norm_apply_forward(
        own_rows.astype(jnp.float32) + hidden, first_gain, first_shift
    )
    grouped = normed_one_out.astype(jnp.bfloat16).reshape(
        seq_count, half_len, GROUPS, features // GROUPS
    )
    up_proj = (
        jnp.einsum("slgi,gio->slgo", grouped, up_weight, preferred_element_type=jnp.float32)
        + up_bias
    )
    active = gelu_exact(up_proj).astype(jnp.bfloat16)
    lowered = (
        jnp.einsum("slgo,goi->slgi", active, down_weight, preferred_element_type=jnp.float32)
        + down_bias
    )
    result, normed_two, inverse_two = norm_apply_forward(
        normed_one_out + lowered.reshape(seq_count, half_len, features), second_gain, second_shift
    )
    activations = result.astype(jnp.bfloat16)
    grad_out = cotangent.astype(jnp.float32)
    second_gain_grad = jnp.sum(grad_out * normed_two, axis=(0, 1))
    second_shift_grad = jnp.sum(grad_out, axis=(0, 1))
    resid_two = norm_backward(grad_out, normed_two, inverse_two, second_gain)
    lowered_grad = resid_two.astype(jnp.bfloat16).reshape(
        seq_count, half_len, GROUPS, features // GROUPS
    )
    down_bias_grad = jnp.sum(lowered_grad.astype(jnp.float32), axis=(0, 1))
    down_weight_grad = jnp.einsum(
        "slgo,slgi->goi", active, lowered_grad, preferred_element_type=jnp.float32
    )
    active_grad = jnp.einsum(
        "slgi,goi->slgo", lowered_grad, down_weight, preferred_element_type=jnp.float32
    )
    gelu_value, gelu_pull = jax.vjp(gelu_exact, up_proj)
    up_grad = gelu_pull(active_grad)[0].astype(jnp.bfloat16)
    up_bias_grad = jnp.sum(up_grad.astype(jnp.float32), axis=(0, 1))
    up_weight_grad = jnp.einsum(
        "slgi,slgo->gio", grouped, up_grad, preferred_element_type=jnp.float32
    )
    norm_one_grad = resid_two + jnp.einsum(
        "slgo,gio->slgi", up_grad, up_weight, preferred_element_type=jnp.float32
    ).reshape(seq_count, half_len, features)
    first_gain_grad = jnp.sum(norm_one_grad * normed_one, axis=(0, 1))
    first_shift_grad = jnp.sum(norm_one_grad, axis=(0, 1))
    resid_one = norm_backward(norm_one_grad, normed_one, inverse_one, first_gain)
    hidden_grad = resid_one.astype(jnp.bfloat16)
    output_bias_grad = jnp.sum(hidden_grad.astype(jnp.float32), axis=(0, 1))
    output_weight_grad = outer_sum(joined_parts, hidden_grad)
    concat_grad = matmul_back(hidden_grad, output_weight).astype(jnp.bfloat16)
    branch_grad = lax.all_to_all(concat_grad, "branch", split_axis=2, concat_axis=1, tiled=True)

    def attention_grads(unused_in):
        key_rows = matmul(inputs, own_weights[0]).astype(jnp.bfloat16)
        value_rows = (matmul(inputs, own_weights[1]) + value_bias).astype(jnp.bfloat16)
        query_part, input_slice, stack_grad, value_bias_grad = attention_backward(
            inputs, queries, key_rows, value_rows, segments, log_totals, branch_grad, own_weights
        )
        return (
            query_part,
            input_slice,
            stack_grad,
            value_bias_grad,
            jnp.zeros(depthwise.shape, jnp.float32),
            jnp.zeros(point_bias.shape, jnp.float32),
            jnp.zeros(kernel_weight.shape, jnp.float32),
            jnp.zeros(kernel_bias.shape, jnp.float32),
            jnp.zeros(conv_bias.shape, jnp.float32),
        )

    def conv_grads(unused_in):
        (
            query_part,
            input_slice,
            stack_grad,
            depthwise_kernel_gradient,
            point_bias_grad,
            kernel_weight_grad,
            kernel_bias_grad,
            conv_bias_grad,
        ) = conv_backward(
            inputs,
            inputs_f,
            queries,
            segments,
            own_weights,
            depthwise,
            point_bias,
            kernel_weight,
            kernel_bias,
            conv_bias,
            branch_grad,
        )
        return (
            query_part,
            input_slice,
            stack_grad,
            jnp.zeros(value_bias.shape, jnp.float32),
            depthwise_kernel_gradient,
            point_bias_grad,
            kernel_weight_grad,
            kernel_bias_grad,
            conv_bias_grad,
        )

    (
        query_part,
        input_slice,
        stack_grad,
        value_bias_grad,
        depthwise_kernel_gradient,
        point_bias_grad,
        kernel_weight_grad,
        kernel_bias_grad,
        conv_bias_grad,
    ) = lax.cond(branch_side == 0, attention_grads, conv_grads, inputs)
    received_query, received_input = (
        lax.all_to_all(
            query_part[None].astype(jnp.bfloat16), "branch", split_axis=2, concat_axis=0, tiled=True
        ).astype(jnp.float32),
        lax.all_to_all(
            shortened(input_slice[None]), "branch", split_axis=2, concat_axis=0, tiled=True
        ),
    )
    query_low = (received_query[0] + received_query[1]).astype(jnp.bfloat16)
    query_bias_grad = jnp.sum(query_low.astype(jnp.float32), axis=(0, 1))
    query_weight_grad = outer_sum(own_rows, query_low)
    input_grad = (
        resid_one + received_input[0] + received_input[1] + matmul_back(query_low, query_weight)
    )
    stack_total = lax.psum(stack_grad, "dp")
    (
        query_weight_grad,
        query_bias_grad,
        value_bias_grad,
        depthwise_kernel_gradient,
        point_bias_grad,
        kernel_weight_grad,
        kernel_bias_grad,
        conv_bias_grad,
        output_weight_grad,
        output_bias_grad,
        first_gain_grad,
        first_shift_grad,
        up_weight_grad,
        up_bias_grad,
        down_weight_grad,
        down_bias_grad,
        second_gain_grad,
        second_shift_grad,
    ) = lax.psum(
        (
            query_weight_grad,
            query_bias_grad,
            value_bias_grad,
            depthwise_kernel_gradient,
            point_bias_grad,
            kernel_weight_grad,
            kernel_bias_grad,
            conv_bias_grad,
            output_weight_grad,
            output_bias_grad,
            first_gain_grad,
            first_shift_grad,
            up_weight_grad,
            up_bias_grad,
            down_weight_grad,
            down_bias_grad,
            second_gain_grad,
            second_shift_grad,
        ),
        ("branch", "dp"),
    )
    return (
        activations,
        input_grad,
        query_weight_grad,
        query_bias_grad,
        stack_total[None],
        value_bias_grad,
        depthwise_kernel_gradient,
        point_bias_grad,
        kernel_weight_grad,
        kernel_bias_grad,
        conv_bias_grad,
        output_weight_grad,
        output_bias_grad,
        first_gain_grad,
        first_shift_grad,
        up_weight_grad,
        up_bias_grad,
        down_weight_grad,
        down_bias_grad,
        second_gain_grad,
        second_shift_grad,
    )


def solution(mesh):
    placed = (
        P("dp", None, None),
        P("dp", None),
        P(),
        P(),
        P("branch", None, None, None),
        P(),
        P(),
        P(),
        P(),
        P(),
        P(),
        P(),
        P(),
        P(),
        P(),
        P(),
        P(),
        P(),
        P(),
        P(),
        P(),
        P("dp", "branch", None),
    )
    return jax.shard_map(
        local,
        mesh=mesh,
        in_specs=placed,
        out_specs=(
            P("dp", "branch", None),
            P("dp", "branch", None),
            P(),
            P(),
            P("branch", None, None, None),
            P(),
            P(),
            P(),
            P(),
            P(),
            P(),
            P(),
            P(),
            P(),
            P(),
            P(),
            P(),
            P(),
            P(),
            P(),
            P(),
        ),
        check_vma=False,
    )
```

profile of v0, /device:TPU:0, one launch (start us, length us, event | category | flops | bytes accessed | tf_op | source)
XLA Modules:
  0.0 929.1 jit_solution(13368890381936245872)
XLA Ops:
  18.9 108.5 %conditional.2 = (bf16[2,1024,384]{1,2,0:T(8,128)(2,1)}, f32[2,2,6,512]{3,2,1,0:T(8,128)}) conditional(s32[]{:T(128)} %convert_element_type.355, (f32[9,768]{1,0:T(8,128)S(1)}, f32[2,1024,768]{2,1,0:T(8,128)}, s32[2,1024]{1,0:T(2,128)S(1)}, bf16[2,768,384]{1,2,0:T(8,128)(2,1)S(1)}, f32[384]{0:T(512)}, /*index=5*/bf16[2,1024,384]{2,1,0:T(8,128)(2,1)}, ...), branch_computations={%region_0.3_spmd, %region_3.8_spmd} | conditional | flops 4105824256 | bytes 224245520 | solution.py:369
  37.7 81.6 %while.25 = (s32[]{:T(128)}, bf16[2,2,512,6,64]{2,4,3,1,0:T(8,128)(2,1)}, f32[2,2,6,512]{3,2,1,0:T(8,128)}, s32[2,2,512]{2,1,0:T(2,128)S(1)}, s32[2,1024]{1,0:T(...) while((s32[]{:T(128)}, ...), condition=%wide.region_7.7_spmd, body=%wide.region_4.6_spmd.sunk | while | flops 1687545856 | bytes 197898416 | solution.py:113
  38.3 14.6 %fusion.290 = (f32[2,6,512]{2,1,0:T(8,128)S(1)}, f32[2,6,512,1024]{3,2,1,0:T(8,128)}) fusion(pred[2,512,1024]{2,1,0:T(8,128)(4,1)S(1)} %broadcast_compare_fusion.5, bf16[2,1024,6,64]{1,3,2,0:T(8,128)(2,1)} %get-tuple-element.863, bf16[2,2,512,6,64]{2,4,3,1,0:T(8,128)(2,1)} %get-tuple-element.862, s32[]{:T(128)S(6)} %copy.422), kind=kOutput, calls=%fused_computation.3.clone.1 | convolution fusion | flops 824174592 | bytes 28598276 | tf_op jit(solution)/shard_map/cond/branch_1_fun/while/body/eval_jaxpr/sqhe,skhe->shqk/dot_general | solution.py:86
  52.9 13.3 %fusion.291 = f32[2,6,512]{2,1,0:T(8,128)S(1)} fusion(f32[2,6,512,1024]{3,2,1,0:T(8,128)} %get-tuple-element.798, f32[2,6,512]{2,1,0:T(8,128)S(1)} %get-tuple-element.799, pred[2,512,1024]{2,1,0:T(8,128)(4,1)S(1)} %broadcast_compare_fusion.5), kind=kLoop, calls=%fused_computation.4.clone.1 | loop fusion | flops 25159680 | bytes 26263552 | tf_op jit(solution)/shard_map/cond/branch_1_fun/while/body/eval_jaxpr/reduce_sum | solution.py:106
  79.2 14.6 %fusion.290 = (f32[2,6,512]{2,1,0:T(8,128)S(1)}, f32[2,6,512,1024]{3,2,1,0:T(8,128)}) fusion(pred[2,512,1024]{2,1,0:T(8,128)(4,1)S(1)} %broadcast_compare_fusion.5, bf16[2,1024,6,64]{1,3,2,0:T(8,128)(2,1)} %get-tuple-element.863, bf16[2,2,512,6,64]{2,4,3,1,0:T(8,128)(2,1)} %get-tuple-element.862, s32[]{:T(128)S(6)} %copy.422), kind=kOutput, calls=%fused_computation.3.clone.1 | convolution fusion | flops 824174592 | bytes 28598276 | tf_op jit(solution)/shard_map/cond/branch_1_fun/while/body/eval_jaxpr/sqhe,skhe->shqk/dot_general | solution.py:86
  93.8 13.3 %fusion.291 = f32[2,6,512]{2,1,0:T(8,128)S(1)} fusion(f32[2,6,512,1024]{3,2,1,0:T(8,128)} %get-tuple-element.798, f32[2,6,512]{2,1,0:T(8,128)S(1)} %get-tuple-element.799, pred[2,512,1024]{2,1,0:T(8,128)(4,1)S(1)} %broadcast_compare_fusion.5), kind=kLoop, calls=%fused_computation.4.clone.1 | loop fusion | flops 25159680 | bytes 26263552 | tf_op jit(solution)/shard_map/cond/branch_1_fun/while/body/eval_jaxpr/reduce_sum | solution.py:106
  137.0 20.2 %all-to-all-done = bf16[2,1024,384]{2,0,1:T(2,128)(2,1)} async-done(((bf16[2,1024,384]{2,0,1:T(2,128)(2,1)}), bf16[2,1024,384]{2,0,1:T(2,128)(2,1)}, u32[]{:S(2)}, u32[]{:S(2)}) %all-to-all-start) | async-done | bytes 1572896 | tf_op jit(solution)/shard_map/all_to_all | solution.py:370
  182.7 33.5 %fusion.159 = (bf16[2,512,2,1536]{3,1,0,2:T(8,128)(2,1)S(1)}, f32[2,512,2,1536]{3,1,0,2:T(8,128)}, f32[2,2,512,1536]{3,2,1,0:T(8,128)}) fusion(f32[2,1536]{1,0:T(2,128)} %param.46, bf16[2,512,2,384]{1,3,0,2:T(8,128)(2,1)} %copy.308, bf16[2,384,1536]{2,1,0:T(8,128)(2,1)S(1)} %copy-done), kind=kOutput, calls=%fused_computation.352 | convolution fusion | flops 2623537152 | bytes 35401728 | tf_op jit(solution)/shard_map/slgi,gio->slgo/dot_general | solution.py:380
  245.1 16.3 %convert_reduce_fusion.4 = (f32[2,1536]{1,0:T(2,128)}, bf16[2,512,2,1536]{3,1,0,2:T(8,128)(2,1)}) fusion(f32[2,512,2,1536]{3,1,0,2:T(8,128)} %get-tuple-element.609, bf16[2,1536,384]{2,1,0:T(8,128)(2,1)S(1)} %copy-done.137, bf16[2,64,2,8,384]{4,3,2,1,0:T(8,128)(2,1)S(1)} %bitcast.514, f32[2,2,512,1536]{3,2,1,0:T(8,128)} %get-tuple-element.671, ...), kind=kOutput, calls=%fused_computation.353 | convolution fusion | flops 2469393408 | bytes 35414016 | tf_op jit(solution)/shard_map/slgi,goi->slgo/dot_general | solution.py:403
  307.2 10.4 %all-to-all-done.1 = bf16[2,512,768]{1,0,2:T(2,128)(2,1)S(1)} async-done(((bf16[2,512,768]{1,0,2:T(2,128)(2,1)}), bf16[2,512,768]{1,0,2:T(2,128)(2,1)S(1)}, u32[]{:S(2)}, u32[]{:S(2)}) %all-to-all-start.1) | async-done | bytes 1572896 | tf_op jit(solution)/shard_map/all_to_all | solution.py:422
  326.8 236.5 %conditional.3 = (bf16[2,1024,384]{2,1,0:T(8,128)(2,1)}, f32[2,768,384]{2,1,0:T(8,128)}, f32[384]{0:T(512)S(1)}, f32[9,768]{1,0:T(8,128)S(1)}, f32[384]{0:T(512)...) conditional(s32[]{:T(128)} %convert_element_type.355, ...), branch_computations={%region_16.41_spmd, %region_41.46_spmd} | conditional | flops 11380123648 | bytes 445177728 | solution.py:487
  352.3 175.3 %while.26 = (s32[]{:T(128)}, f32[2,1024,6,64]{1,3,2,0:T(8,128)}, f32[2,1024,6,64]{1,3,2,0:T(8,128)}, bf16[2,2,512,6,64]{2,4,3,1,0:T(8,128)(2,1)}, bf16[2,2,512,6...) while((s32[]{:T(128)}, f32[2,1024,6,64]{1,3,2,0:T(8,128)}, ...), condition=%wide.region_44.44_spmd.clone, body=%wide.region_42.43_spmd.clone.sunk | while | flops 4125485056 | bytes 227741904 | solution.py:156
  354.2 13.5 %fusion.287 = f32[2,6,512,1024]{3,2,1,0:T(8,128)} fusion(bf16[2,1024,6,64]{1,3,2,0:T(8,128)(2,1)} %get-tuple-element.833, bf16[2,2,512,6,64]{2,4,3,1,0:T(8,128)(2,1)} %get-tuple-element.830, s32[]{:T(128)S(6)} %copy.409), kind=kOutput, calls=%fused_computation.38.clone.1 | convolution fusion | flops 805306368 | bytes 27525124 | tf_op jit(solution)/shard_map/cond/branch_1_fun/while/body/eval_jaxpr/sqhe,skhe->shqk/dot_general | solution.py:86
  367.7 13.7 %bitcast_add_fusion.5 = f32[2,1024,6,64]{1,3,2,0:T(8,128)} fusion(f32[2,1024,6,64]{1,3,2,0:T(8,128)} %get-tuple-element.815, f32[2,6,512,1024]{3,2,1,0:T(8,128)} %fusion.287, f32[2,6,512]{2,1,0:T(8,128)S(1)} %dynamic-slice_bitcast_fusion.6, pred[2,512,1024]{2,1,0:T(8,128)(4,1)S(1)} %broadcast_compare_fusion.4, pred[]{:T(512)S(6)} %compare.25, ...), kind=kOutput, calls=%fused_computation.30.clone.1 | convolution fusion | flops 832045056 | bytes 33325060 | tf_op jit(solution)/shard_map/cond/branch_1_fun/while/body/eval_jaxpr/shqk,sqhe->skhe/dot_general | solution.py:134
  381.4 18.2 %multiply_reduce_fusion.17 = (f32[2,6,512]{2,1,0:T(8,128)S(1)}, f32[2,6,512,1024]{3,2,1,0:T(8,128)}) fusion(f32[2,6,512,1024]{3,2,1,0:T(8,128)} %fusion.287, f32[2,6,512]{2,1,0:T(8,128)S(1)} %dynamic-slice_bitcast_fusion.6, pred[2,512,1024]{2,1,0:T(8,128)(4,1)S(1)} %broadcast_compare_fusion.4, bf16[2,1024,6,64]{1,3,2,0:T(8,128)(2,1)} %get-tuple-element.836, ...), kind=kOutput, calls=%fused_computation.25.clone.1 | convolution fusion | flops 836757504 | bytes 53788676 | tf_op jit(solution)/shard_map/cond/branch_1_fun/while/body/eval_jaxpr/sqhe,skhe->shqk/dot_general | solution.py:140
  399.6 21.1 %multiply_convert_fusion.7 = bf16[2,6,512,1024]{3,2,1,0:T(8,128)(2,1)} fusion(f32[2,6,512,1024]{3,2,1,0:T(8,128)} %get-tuple-element.788, f32[2,6,512,1024]{3,2,1,0:T(8,128)} %fusion.287, f32[2,6,512]{2,1,0:T(8,128)S(1)} %get-tuple-element.789, f32[2,6,512]{2,1,0:T(8,128)S(1)} %dynamic-slice_bitcast_fusion.6, ...), kind=kLoop, calls=%fused_computation.24.clone.1 | loop fusion | flops 37748736 | bytes 64012288 | tf_op jit(solution)/shard_map/cond/branch_1_fun/while/body/eval_jaxpr/convert_element_type | solution.py:145
  420.7 9.9 %bitcast_dynamic-update-slice_fusion.4 = bf16[2,2,512,6,64]{2,4,3,1,0:T(8,128)(2,1)} fusion(bf16[2,2,512,6,64]{2,4,3,1,0:T(8,128)(2,1)} %get-tuple-element.816, s32[]{:T(128)S(6)} %copy.409, bf16[2,6,512,1024]{3,2,1,0:T(8,128)(2,1)} %multiply_convert_fusion.7, bf16[2,1024,6,64]{1,3,2,0:T(8,128)(2,1)} %get-tuple-element.833), kind=kOutput, calls=%fused_computation.33.clone.1 | convolution fusion | flops 805699584 | bytes 15728644 | tf_op jit(solution)/shard_map/cond/branch_1_fun/while/body/eval_jaxpr/shqk,skhe->sqhe/dot_general | solution.py:147
  440.6 13.5 %fusion.287 = f32[2,6,512,1024]{3,2,1,0:T(8,128)} fusion(bf16[2,1024,6,64]{1,3,2,0:T(8,128)(2,1)} %get-tuple-element.833, bf16[2,2,512,6,64]{2,4,3,1,0:T(8,128)(2,1)} %get-tuple-element.830, s32[]{:T(128)S(6)} %copy.409), kind=kOutput, calls=%fused_computation.38.clone.1 | convolution fusion | flops 805306368 | bytes 27525124 | tf_op jit(solution)/shard_map/cond/branch_1_fun/while/body/eval_jaxpr/sqhe,skhe->shqk/dot_general | solution.py:86
  454.1 14.7 %bitcast_add_fusion.5 = f32[2,1024,6,64]{1,3,2,0:T(8,128)} fusion(f32[2,1024,6,64]{1,3,2,0:T(8,128)} %get-tuple-element.815, f32[2,6,512,1024]{3,2,1,0:T(8,128)} %fusion.287, f32[2,6,512]{2,1,0:T(8,128)S(1)} %dynamic-slice_bitcast_fusion.6, pred[2,512,1024]{2,1,0:T(8,128)(4,1)S(1)} %broadcast_compare_fusion.4, pred[]{:T(512)S(6)} %compare.25, ...), kind=kOutput, calls=%fused_computation.30.clone.1 | convolution fusion | flops 832045056 | bytes 33325060 | tf_op jit(solution)/shard_map/cond/branch_1_fun/while/body/eval_jaxpr/shqk,sqhe->skhe/dot_general | solution.py:134
  468.8 18.2 %multiply_reduce_fusion.17 = (f32[2,6,512]{2,1,0:T(8,128)S(1)}, f32[2,6,512,1024]{3,2,1,0:T(8,128)}) fusion(f32[2,6,512,1024]{3,2,1,0:T(8,128)} %fusion.287, f32[2,6,512]{2,1,0:T(8,128)S(1)} %dynamic-slice_bitcast_fusion.6, pred[2,512,1024]{2,1,0:T(8,128)(4,1)S(1)} %broadcast_compare_fusion.4, bf16[2,1024,6,64]{1,3,2,0:T(8,128)(2,1)} %get-tuple-element.836, ...), kind=kOutput, calls=%fused_computation.25.clone.1 | convolution fusion | flops 836757504 | bytes 53788676 | tf_op jit(solution)/shard_map/cond/branch_1_fun/while/body/eval_jaxpr/sqhe,skhe->shqk/dot_general | solution.py:140
  487.0 21.1 %multiply_convert_fusion.7 = bf16[2,6,512,1024]{3,2,1,0:T(8,128)(2,1)} fusion(f32[2,6,512,1024]{3,2,1,0:T(8,128)} %get-tuple-element.788, f32[2,6,512,1024]{3,2,1,0:T(8,128)} %fusion.287, f32[2,6,512]{2,1,0:T(8,128)S(1)} %get-tuple-element.789, f32[2,6,512]{2,1,0:T(8,128)S(1)} %dynamic-slice_bitcast_fusion.6, ...), kind=kLoop, calls=%fused_computation.24.clone.1 | loop fusion | flops 37748736 | bytes 64012288 | tf_op jit(solution)/shard_map/cond/branch_1_fun/while/body/eval_jaxpr/convert_element_type | solution.py:145
  508.1 9.9 %bitcast_dynamic-update-slice_fusion.4 = bf16[2,2,512,6,64]{2,4,3,1,0:T(8,128)(2,1)} fusion(bf16[2,2,512,6,64]{2,4,3,1,0:T(8,128)(2,1)} %get-tuple-element.816, s32[]{:T(128)S(6)} %copy.409, bf16[2,6,512,1024]{3,2,1,0:T(8,128)(2,1)} %multiply_convert_fusion.7, bf16[2,1024,6,64]{1,3,2,0:T(8,128)(2,1)} %get-tuple-element.833), kind=kOutput, calls=%fused_computation.33.clone.1 | convolution fusion | flops 805699584 | bytes 15728644 | tf_op jit(solution)/shard_map/cond/branch_1_fun/while/body/eval_jaxpr/shqk,skhe->sqhe/dot_general | solution.py:147
  609.6 68.8 %all-reduce.22 = (f32[384]{0:T(512)}, f32[384]{0:T(512)}, f32[9,768]{1,0:T(8,128)}, f32[384]{0:T(512)}, f32[54]{0:T(128)}, /*index=5*/f32[384]{0:T(512)}, f32[76...) all-reduce(f32[384]{0:T(512)S(1)} %get-tuple-element.603, ...), channel_id=1, replica_groups=mesh['branch'=2,'dp'=16] {'branch','dp'}, use_global_device_ids=true, to_apply=%region_48.49 | all-reduce | flops 16182 | bytes 129456 | tf_op jit(solution)/shard_map/psum | solution.py:522
  685.2 225.0 %all-reduce.29.cloned.1.call-done = (f32[768,384]{1,0:T(8,128)}, f32[384,54]{0,1:T(8,128)}, f32[768,768]{1,0:T(8,128)}, f32[2,384,1536]{2,1,0:T(8,128)}, f32[2,1536,384]{2,1,0:T(8,128)}) async-done(((f32[768,384]{1,0:T(8,128)}, f32[384,54]{0,1:T(8,128)}, f32[768,768]{1,0:T(8,128)}, f32[2,384,1536]{2,1,0:T(8,128)}, f32[2,1536,384]{2,1,0:T(8,128)}), (f32[768,384]{1,0:T(8,128)}, f32[384,54]{0,1:T(8,128)}, ...) | async-done | bytes 13059088 | tf_op jit(solution)/shard_map/psum | solution.py:522
  (300 shorter events, 325.4 us)
Async XLA Ops:
  7.2 175.5 %copy-start = (bf16[2,384,1536]{2,1,0:T(8,128)(2,1)S(1)}, bf16[2,384,1536]{2,1,0:T(8,128)(2,1)}, u32[]{:S(2)}) copy-start(bf16[2,384,1536]{2,1,0:T(8,128)(2,1)} %param.45) | copy-start | bytes 7077892
  38.3 27.9 %copy-start.38 = (bf16[2,2,512,6,64]{2,4,3,1,0:T(8,128)(2,1)S(1)}, bf16[2,2,512,6,64]{2,4,3,1,0:T(8,128)(2,1)}, u32[]{:S(2)}) copy-start(bf16[2,2,512,6,64]{2,4,3,1,0:T(8,128)(2,1)} %get-tuple-element.849) | copy-start | bytes 4718596 | tf_op jit(solution)/shard_map/cond/branch_1_fun/while
  52.9 15.5 %copy-start.2 = (f32[2,6,512,1024]{3,2,1,0:T(8,128)S(1)}, f32[2,6,512,1024]{3,2,1,0:T(8,128)}, u32[]{:S(2)}) copy-start(f32[2,6,512,1024]{3,2,1,0:T(8,128)} %get-tuple-element.798) | copy-start | bytes 75497472 | tf_op jit(solution)/shard_map/cond/branch_1_fun/while
  79.1 27.9 %copy-start.38 = (bf16[2,2,512,6,64]{2,4,3,1,0:T(8,128)(2,1)S(1)}, bf16[2,2,512,6,64]{2,4,3,1,0:T(8,128)(2,1)}, u32[]{:S(2)}) copy-start(bf16[2,2,512,6,64]{2,4,3,1,0:T(8,128)(2,1)} %get-tuple-element.849) | copy-start | bytes 4718596 | tf_op jit(solution)/shard_map/cond/branch_1_fun/while
  93.8 15.5 %copy-start.2 = (f32[2,6,512,1024]{3,2,1,0:T(8,128)S(1)}, f32[2,6,512,1024]{3,2,1,0:T(8,128)}, u32[]{:S(2)}) copy-start(f32[2,6,512,1024]{3,2,1,0:T(8,128)} %get-tuple-element.798) | copy-start | bytes 75497472 | tf_op jit(solution)/shard_map/cond/branch_1_fun/while
  132.4 24.8 %all-to-all-start = ((bf16[2,1024,384]{2,0,1:T(2,128)(2,1)}), bf16[2,1024,384]{2,0,1:T(2,128)(2,1)}, u32[]{:S(2)}, u32[]{:S(2)}) async-start(bf16[2,1024,384]{2,0,1:T(2,128)(2,1)} %copy.290), calls=%async_computation | async-start | bytes 3145728 | tf_op jit(solution)/shard_map/all_to_all | solution.py:370
  170.1 117.1 %copy-start.66 = (f32[2,512]{1,0:T(2,128)}, f32[2,512]{1,0:T(2,128)S(1)}, u32[]{:S(2)}) copy-start(f32[2,512]{1,0:T(2,128)S(1)} %broadcast_multiply_fusion.5) | copy-start | bytes 12292
  171.7 115.5 %copy-start.74 = (f32[2,512]{1,0:T(2,128)}, f32[2,512]{1,0:T(2,128)S(1)}, u32[]{:S(2)}) copy-start(f32[2,512]{1,0:T(2,128)S(1)} %add_rsqrt_fusion.1) | copy-start | bytes 12292
  182.7 36.2 %copy-start.136 = (bf16[2,1536,384]{2,1,0:T(8,128)(2,1)S(1)}, bf16[2,1536,384]{2,1,0:T(8,128)(2,1)}, u32[]{:S(2)}) copy-start(bf16[2,1536,384]{2,1,0:T(8,128)(2,1)} %param.47) | copy-start | bytes 7077892
  182.7 36.2 %copy-start.143 = (f32[2,384]{1,0:T(2,128)S(1)}, f32[2,384]{1,0:T(2,128)}, u32[]{:S(2)}) copy-start(f32[2,384]{1,0:T(2,128)} %param.48) | copy-start | bytes 9220
  245.0 16.4 %copy-start.41 = (bf16[2,512,768]{2,1,0:T(8,128)(2,1)}, bf16[2,512,768]{2,1,0:T(8,128)(2,1)S(1)}, u32[]{:S(2)}) copy-start(bf16[2,512,768]{2,1,0:T(8,128)(2,1)S(1)} %get-tuple-element.600) | copy-start | bytes 4718596
  294.6 23.0 %all-to-all-start.1 = ((bf16[2,512,768]{1,0,2:T(2,128)(2,1)}), bf16[2,512,768]{1,0,2:T(2,128)(2,1)S(1)}, u32[]{:S(2)}, u32[]{:S(2)}) async-start(bf16[2,512,768]{1,0,2:T(2,128)(2,1)} %copy.297), calls=%async_computation.1 | async-start | bytes 3145728 | tf_op jit(solution)/shard_map/all_to_all | solution.py:422
  298.2 387.0 %all-reduce.27.cloned.1.call-start = ((), (), s32[]{:S(2)}) async-start(), calls=%async_computation.4 | async-start | bytes 4718592 | tf_op jit(solution)/shard_map/psum | solution.py:502
  330.2 17.6 %copy-start.12 = (bf16[2,768,384]{1,2,0:T(8,128)(2,1)}, bf16[2,768,384]{1,2,0:T(8,128)(2,1)S(1)}, u32[]{:S(2)}) copy-start(bf16[2,768,384]{1,2,0:T(8,128)(2,1)S(1)} %get-tuple-element.204) | copy-start | bytes 3538948 | tf_op jit(solution)/shard_map/cond
  567.6 22.1 %all-to-all-start.3 = ((bf16[1,2,1024,384]{3,1,0,2:T(2,128)(2,1)}), bf16[1,2,1024,384]{3,1,0,2:T(2,128)(2,1)S(1)}, u32[]{:S(2)}, u32[]{:S(2)}) async-start(bf16[1,2,1024,384]{3,1,0,2:T(2,128)(2,1)} %bitcast.421), calls=%async_computation.3 | async-start | bytes 3145728 | tf_op jit(solution)/shard_map/all_to_all | solution.py:489
  571.3 338.9 %all-reduce.29.cloned.1.call-start = ((), (), s32[]{:S(2)}) async-start(), calls=%async_computation.5 | async-start | bytes 26124288 | tf_op jit(solution)/shard_map/psum | solution.py:522
  604.1 76.8 %copy-start.67 = (f32[2,512]{1,0:T(2,128)S(1)}, f32[2,512]{1,0:T(2,128)}, u32[]{:S(2)}) copy-start(f32[2,512]{1,0:T(2,128)} %copy-done.66) | copy-start | bytes 12292
  604.1 76.8 %copy-start.75 = (f32[2,512]{1,0:T(2,128)S(1)}, f32[2,512]{1,0:T(2,128)}, u32[]{:S(2)}) copy-start(f32[2,512]{1,0:T(2,128)} %copy-done.74) | copy-start | bytes 12292
  604.1 76.8 %copy-start.81 = (f32[768]{0:T(1024)S(1)}, f32[768]{0:T(1024)}, u32[]{:S(2)}) copy-start(f32[768]{0:T(1024)} %param.43) | copy-start | bytes 9220
  604.1 76.8 %copy-start.121 = (f32[2,512]{1,0:T(2,128)S(1)}, f32[2,512]{1,0:T(2,128)}, u32[]{:S(2)}) copy-start(f32[2,512]{1,0:T(2,128)} %copy-done.120) | copy-start | bytes 12292
  604.1 76.8 %copy-start.123 = (f32[2,512]{1,0:T(2,128)S(1)}, f32[2,512]{1,0:T(2,128)}, u32[]{:S(2)}) copy-start(f32[2,512]{1,0:T(2,128)} %copy-done.122) | copy-start | bytes 12292
  604.1 76.8 %copy-start.140 = (bf16[768,384]{1,0:T(8,128)(2,1)S(1)}, bf16[768,384]{1,0:T(8,128)(2,1)}, u32[]{:S(2)}) copy-start(bf16[768,384]{1,0:T(8,128)(2,1)} %param.32) | copy-start | bytes 1769476
  604.1 74.3 %all-to-all-start.2 = ((bf16[1,2,1024,768]{3,1,0,2:T(2,128)(2,1)}), bf16[1,2,1024,768]{3,1,0,2:T(2,128)(2,1)}, u32[]{:S(2)}, u32[]{:S(2)}) async-start(bf16[1,2,1024,768]{3,1,0,2:T(2,128)(2,1)} %copy.301), calls=%async_computation.2 | async-start | bytes 6291456 | tf_op jit(solution)/shard_map/all_to_all | solution.py:492
  685.2 227.6 %copy-start.35 = (f32[1,2,768,384]{3,2,1,0:T(8,128)S(1)}, f32[1,2,768,384]{3,2,1,0:T(8,128)}, u32[]{:S(2)}) copy-start(f32[1,2,768,384]{3,2,1,0:T(8,128)} %all-reduce.27.cloned.1.call-done) | copy-start | bytes 7077892
  (74 other events, 362.4 us)
Sparse Core Ops, SparseCore 0:
  563.5 99.7 all-reduce.26
  671.4 238.8 all-reduce.28
where the time goes:
time: 934 us; the launch traced here: 929 us
  matrix products  311 us (33%)
  waiting for transfers between devices  262 us (28%)
  local copies, waits for them, and re-layouts  141 us (15%)
  other arithmetic  109 us (12%)
  blocking collectives  68.8 us (7%)
  starting transfers between devices  17.5 us (2%)
  between operations  15.1 us (2%)
    psum x1, waiting for transfers between devices, local(): lax.psum((query_weight_grad, query_bias_grad, value_bias_grad, depthwise_...  225 us
    psum x1, blocking collectives, local(): lax.psum((query_weight_grad, query_bias_grad, value_bias_grad, depthwise_...  68.8 us
    dot_general x4, matrix products, attention_scores(): jnp.einsum('sqhe,skhe->shqk', query_block, key_heads, preferred_element_t...  56.3 us
    convert_element_type x2, other arithmetic, one_block(): score_grad = (row_probs * (prob_grad - jnp.sum(row_probs * prob_grad, axi...  42.2 us
    dot_general x2, matrix products, one_block(): jnp.einsum('sqhe,skhe->shqk', grad_block, value_heads, preferred_element_...  36.5 us
    dot_general x1, matrix products, local(): jnp.einsum('slgi,gio->slgo', grouped, up_weight, preferred_element_type=j...  33.5 us
    dot_general x2, matrix products, one_block(): jnp.einsum('shqk,sqhe->skhe', row_probs.astype(jnp.bfloat16), grad_block,...  28.4 us
    unnamed x162, local copies, waits for them, and re-layouts  27.5 us
  transfers between devices with their start and end apart: 6, of which 4 were waited for; matrix products, arithmetic and copies ran while one was open for 5% of the time, Pallas kernels for 0%

commit v1 on v0

v1 whole, which is shorter than its diff:
```python
import jax
import jax.numpy as jnp
from jax import lax
from jax.experimental import pallas as pl
from jax.experimental.pallas import tpu as pltpu
from jax.sharding import PartitionSpec as P

HEADS = 6
HEAD = 64
KERNEL = 9
HALF = KERNEL // 2
GROUPS = 2
DOCS = 8
EPS = 1e-12
BIG = -1e30
SCALE = HEAD**-0.5

PAD = 16
SLOTS = 10
LANES = 128
f32 = jnp.float32
bf16 = jnp.bfloat16


def mm(a, b):
    return jnp.dot(a, b, preferred_element_type=f32)


def mm_nt(a, b):
    return lax.dot_general(a, b, (((1,), (1,)), ((), ())), preferred_element_type=f32)


def mm_tn(a, b):
    return lax.dot_general(a, b, (((0,), (0,)), ((), ())), preferred_element_type=f32)


def params(mib):
    return pltpu.CompilerParams(vmem_limit_bytes=mib * 1024 * 1024)


def cost(flops, nbytes):
    return pl.CostEstimate(flops=int(flops), bytes_accessed=int(nbytes), transcendentals=0)


def window(ref, start, rows, cols):
    return ref[pl.ds(pl.multiple_of(start + PAD - 8, 8), rows + 16), cols]


def moved(win, offset, rows):
    total = rows + 16
    if offset == 0:
        return win[8 : 8 + rows]
    return pltpu.roll(win, (-offset) % total, 0)[8 : 8 + rows]


def clear_pads(ref, length):
    width = ref.shape[1]
    ref[0:PAD, :] = jnp.zeros((PAD, width), f32)
    ref[PAD + length : PAD + length + PAD, :] = jnp.zeros((PAD, width), f32)


def front_body(x_ref, maskc_ref, wq_ref, bq_ref, dw_ref, q_ref, dl_ref, pad):
    length, width = x_ref.shape
    clear_pads(pad, length)
    rows = 32

    @pl.loop(0, length // 128)
    def _(i):
        t0 = pl.multiple_of(i * 128, 128)
        pad[pl.ds(pl.multiple_of(t0 + PAD, 16), 128), :] = x_ref[pl.ds(t0, 128), :].astype(f32)

    @pl.loop(0, length // 256)
    def _(i):
        t0 = pl.multiple_of(i * 256, 256)
        q_ref[pl.ds(t0, 256), :] = (mm(x_ref[pl.ds(t0, 256), :], wq_ref[...]) + bq_ref[...]).astype(
            bf16
        )

    @pl.loop(0, length // rows)
    def _(i):
        t0 = pl.multiple_of(i * rows, rows)
        mask = maskc_ref[pl.ds(t0, rows), :]
        masks = [jnp.broadcast_to(mask[:, j : j + 1], (rows, LANES)) for j in range(KERNEL)]
        for c in range(width // LANES):
            cols = slice(c * LANES, (c + 1) * LANES)
            win = window(pad, t0, rows, cols)
            total = jnp.zeros((rows, LANES), f32)
            for j in range(KERNEL):
                total = total + dw_ref[j : j + 1, cols] * moved(win, j - HALF, rows) * masks[j]
            dl_ref[pl.ds(t0, rows), cols] = total.astype(bf16)


def front(x, maskc, wq, bq, dw):
    length, width = x.shape
    inner = wq.shape[1]
    return pl.pallas_call(
        front_body,
        out_shape=(
            jax.ShapeDtypeStruct((length, inner), bf16),
            jax.ShapeDtypeStruct((length, width), bf16),
        ),
        scratch_shapes=[pltpu.VMEM((length + 2 * PAD, width), f32)],
        compiler_params=params(40),
        cost_estimate=cost(2e10, 8e6),
        name="front",
    )(x, maskc, wq, bq, dw)


def conv_taps(taps, pad, expand_ref, spread, out_ref, length):
    rows = 32
    block = 256
    inner = out_ref.shape[1]

    @pl.loop(0, length // block)
    def _(b):
        b0 = pl.multiple_of(b * block, block)
        for j in range(KERNEL):
            spread[:, j * inner : (j + 1) * inner] = mm(
                taps[pl.ds(b0, block), :], expand_ref[:, j * inner : (j + 1) * inner]
            )

        @pl.loop(0, block // rows)
        def _(i):
            r0 = pl.multiple_of(i * rows, rows)
            t0 = pl.multiple_of(b0 + r0, rows)
            for c in range(inner // LANES):
                cols = slice(c * LANES, (c + 1) * LANES)
                win = window(pad, t0, rows, cols)
                total = jnp.zeros((rows, LANES), f32)
                for j in range(KERNEL):
                    part = spread[pl.ds(r0, rows), j * inner + c * LANES : j * inner + (c + 1) * LANES]
                    total = total + part * moved(win, j - HALF, rows)
                out_ref[pl.ds(t0, rows), cols] = total.astype(bf16)


def taps_in_rows(low_taps, taps, length):
    stacked = jnp.concatenate(low_taps + [jnp.zeros((LANES - 8 * KERNEL, length), f32)], axis=0)
    for b in range(length // LANES):
        piece = stacked[:, b * LANES : (b + 1) * LANES]
        taps[b * LANES : (b + 1) * LANES, :] = jnp.transpose(piece).astype(bf16)


def mixers_body(
    place_ref, x_ref, q_ref, dl_ref, maskr_ref, own_ref, got_ref, got2_ref, bv_ref, bp_ref, bc_ref,
    kw_ref, kb_ref, expand_ref,
    k_ref, v_ref, kc_ref, cv_ref, probs_ref, mixed_ref, w_ref,
    pad, mixing, taps, spread,
):
    length = x_ref.shape[0]
    clear_pads(pad, length)
    side, core = place_ref[0], place_ref[1]
    for n in range(2):
        w_ref[2 * side + n] = own_ref[n]
    w_ref[2 - 2 * side + core] = got_ref[...]
    w_ref[3 - 2 * side - core] = got2_ref[...]

    @pl.loop(0, length // 256)
    def _(i):
        t0 = pl.multiple_of(i * 256, 256)
        now = pl.ds(t0, 256)
        x = x_ref[now, :]
        cv = (mm(x, w_ref[3]) + bc_ref[...]).astype(bf16)
        cv_ref[now, :] = cv
        pad[pl.ds(pl.multiple_of(t0 + PAD, 16), 256), :] = cv.astype(f32)
        kc = (mm(dl_ref[now, :], w_ref[2]) + bp_ref[...]).astype(bf16)
        kc_ref[now, :] = kc
        mixing[now, :] = (kc.astype(f32) * q_ref[now, :].astype(f32)).astype(bf16)
        k_ref[now, :] = mm(x, w_ref[0]).astype(bf16)
        v_ref[now, :] = (mm(x, w_ref[1]) + bv_ref[...]).astype(bf16)

    logits = mm_nt(kw_ref[...], mixing[...]) + kb_ref[:, 0:1]
    rows = [logits[8 * j : 8 * j + 8, :] for j in range(KERNEL)]
    peak = rows[0]
    for r in rows[1:]:
        peak = jnp.maximum(peak, r)
    powers = [jnp.exp(r - peak) for r in rows]
    whole = powers[0]
    for r in powers[1:]:
        whole = whole + r
    share = 1.0 / whole
    low_taps = []
    for j in range(KERNEL):
        probs = powers[j] * share
        probs_ref[8 * j : 8 * j + 8, :] = probs
        low_taps.append(probs.astype(bf16).astype(f32) * maskr_ref[j : j + 1, :])
    taps_in_rows(low_taps, taps, length)
    conv_taps(taps, pad, expand_ref, spread, mixed_ref, length)


def mixers(place, x, q, dl, maskr, own, got, got2, bv, bp, bc, kw, kb, expand):
    length, width = x.shape
    inner = q.shape[1]
    act = jax.ShapeDtypeStruct((length, inner), bf16)
    vm = pl.BlockSpec(memory_space=pltpu.VMEM)
    return pl.pallas_call(
        mixers_body,
        in_specs=[pl.BlockSpec(memory_space=pltpu.SMEM)] + [vm] * 13,
        out_specs=(vm,) * 7,
        out_shape=(
            act, act, act, act, jax.ShapeDtypeStruct((8 * KERNEL, length), f32), act,
            jax.ShapeDtypeStruct((4, width, inner), bf16),
        ),
        scratch_shapes=[
            pltpu.VMEM((length + 2 * PAD, inner), f32),
            pltpu.VMEM((length, inner), bf16),
            pltpu.VMEM((length, LANES), bf16),
            pltpu.VMEM((256, KERNEL * inner), f32),
        ],
        compiler_params=params(48),
        cost_estimate=cost(2e10, 1e7),
        name="mixers",
    )(place, x, q, dl, maskr, own, got, got2, bv, bp, bc, kw, kb, expand)


def head_lanes(shape, head):
    lane = lax.broadcasted_iota(jnp.int32, shape, 1)
    return (lane < HEAD) if head == 0 else (lane >= HEAD)


def only(pair, head):
    return jnp.where(head_lanes(pair.shape, head), pair, jnp.zeros_like(pair))


def attend_body(q_ref, k_ref, v_ref, segc_ref, o_ref, of_ref, lse_ref, kx, vx, qx):
    length = q_ref.shape[0]
    block = 256
    lane = lax.broadcasted_iota(jnp.int32, (length, LANES), 1)
    seg = segc_ref[:, 0:LANES]
    same = seg == lane
    qx[:, 0:LANES] = (q_ref[...].astype(f32) * SCALE).astype(bf16)
    qx[:, LANES:] = jnp.where(same, 1.0, 0.0).astype(bf16)
    other = jnp.where((lane < DOCS) & jnp.logical_not(same), BIG, 0.0).astype(bf16)
    for h in range(2):
        kx[h, :, 0:LANES] = only(k_ref[...].astype(f32), h).astype(bf16)
        kx[h, :, LANES:] = other
    vx[:, 0:LANES] = v_ref[...]
    vx[:, LANES:] = jnp.ones((length, LANES), bf16)

    @pl.loop(0, length // block)
    def _(i):
        t0 = pl.multiple_of(i * block, block)
        now = pl.ds(t0, block)
        outs, totals = [], []
        for h in range(2):
            scores = mm_nt(qx[now, :], kx[h])
            peak = jnp.max(scores, axis=-1, keepdims=True)
            powers = jnp.exp(scores - peak).astype(bf16)
            both = mm(powers, vx[...])
            whole = both[:, LANES:]
            outs.append(both[:, 0:LANES] / whole)
            totals.append(peak + jnp.log(whole))
        left = head_lanes((block, LANES), 0)
        out = jnp.where(left, outs[0], outs[1])
        of_ref[now, :] = out
        o_ref[now, :] = out.astype(bf16)
        lse_ref[now, :] = jnp.where(left, totals[0], totals[1])


def attend(q, k, v, segc):
    length, inner = q.shape
    pair = pl.BlockSpec((length, LANES), lambda p: (0, p))
    fixed = pl.BlockSpec((length, LANES), lambda p: (0, 0))
    return pl.pallas_call(
        attend_body,
        grid=(inner // LANES,),
        in_specs=[pair, pair, pair, fixed],
        out_specs=(pair, pair, pair),
        out_shape=(
            jax.ShapeDtypeStruct((length, inner), bf16),
            jax.ShapeDtypeStruct((length, inner), f32),
            jax.ShapeDtypeStruct((length, inner), f32),
        ),
        scratch_shapes=[
            pltpu.VMEM((2, length, 2 * LANES), bf16),
            pltpu.VMEM((length, 2 * LANES), bf16),
            pltpu.VMEM((length, 2 * LANES), bf16),
        ],
        compiler_params=params(40),
        cost_estimate=cost(2e10, 1e7),
        name="attend",
    )(q, k, v, segc)


def pieces(value):
    first = value.astype(bf16).astype(f32)
    rest = value - first
    second = rest.astype(bf16).astype(f32)
    return first, second, rest - second


def extra_lanes(base, values, lane):
    out = base
    for n, value in enumerate(values):
        out = jnp.where(lane == DOCS + n, value, out)
    return out


def attend_back_body(
    q_ref, k_ref, v_ref, do_ref, of_ref, lse_ref, segc_ref, dq_ref, dk_ref, dv_ref,
    kx, vx, qx, dx, kt, dk_sum, dv_sum,
):
    length = q_ref.shape[0]
    block = 256
    lane = lax.broadcasted_iota(jnp.int32, (length, LANES), 1)
    seg = segc_ref[:, 0:LANES]
    same = seg == lane
    q = q_ref[...].astype(f32) * SCALE
    k = k_ref[...].astype(f32)
    v = v_ref[...].astype(f32)
    do = do_ref[...].astype(f32)
    dots = do * of_ref[...]
    lses = lse_ref[...]
    here = jnp.where(same, 1.0, 0.0)
    other = jnp.where((lane < DOCS) & jnp.logical_not(same), BIG, 0.0)
    ones = jnp.where((lane >= DOCS) & (lane < DOCS + 3), 1.0, 0.0)
    for h in range(2):
        kx[h, :, 0:LANES] = only(k, h).astype(bf16)
        kx[h, :, LANES:] = (other + ones).astype(bf16)
        vx[h, :, 0:LANES] = only(v, h).astype(bf16)
        vx[h, :, LANES:] = ones.astype(bf16)
        qx[h, :, 0:LANES] = only(q, h).astype(bf16)
        minus = [-p for p in pieces(lses[:, h * HEAD : h * HEAD + 1])]
        qx[h, :, LANES:] = extra_lanes(here, minus, lane).astype(bf16)
        dx[h, :, 0:LANES] = only(do, h).astype(bf16)
        dot = jnp.sum(only(dots, h), axis=-1, keepdims=True)
        minus = [-p for p in pieces(dot)]
        dx[h, :, LANES:] = extra_lanes(jnp.zeros_like(here), minus, lane).astype(bf16)
        kt[h] = jnp.transpose(only(k, h)).astype(bf16)
    dk_sum[...] = jnp.zeros_like(dk_sum)
    dv_sum[...] = jnp.zeros_like(dv_sum)

    @pl.loop(0, length // block)
    def _(i):
        t0 = pl.multiple_of(i * block, block)
        now = pl.ds(t0, block)
        dq = jnp.zeros((LANES, block), f32)
        for h in range(2):
            for b in range(length // block):
                keys = slice(b * block, (b + 1) * block)
                probs = jnp.exp(mm_nt(kx[h, keys, :], qx[h, now, :]))
                grads = mm_nt(vx[h, keys, :], dx[h, now, :])
                score = (probs * grads).astype(bf16)
                dv_sum[keys, :] += mm(probs.astype(bf16), dx[h, now, 0:LANES])
                dk_sum[keys, :] += mm(score, qx[h, now, 0:LANES])
                dq = dq + mm(kt[h, :, keys], score)
        dq_ref[now, :] = jnp.transpose(dq) * SCALE

    dk_ref[...] = dk_sum[...].astype(bf16)
    dv_ref[...] = dv_sum[...].astype(bf16)


def attend_back(pair_no, q, k, v, do, of, lse, segc):
    length, inner = q.shape
    pair = pl.BlockSpec((length, LANES), lambda p: (0, pair_no))
    fixed = pl.BlockSpec((length, LANES), lambda p: (0, 0))
    wide = pltpu.VMEM((2, length, 2 * LANES), bf16)
    return pl.pallas_call(
        attend_back_body,
        grid=(1,),
        in_specs=[pair] * 6 + [fixed],
        out_specs=(fixed, fixed, fixed),
        out_shape=(
            jax.ShapeDtypeStruct((length, LANES), f32),
            jax.ShapeDtypeStruct((length, LANES), bf16),
            jax.ShapeDtypeStruct((length, LANES), bf16),
        ),
        scratch_shapes=[
            wide, wide, wide, wide,
            pltpu.VMEM((2, LANES, length), bf16),
            pltpu.VMEM((length, LANES), f32),
            pltpu.VMEM((length, LANES), f32),
        ],
        compiler_params=params(48),
        cost_estimate=cost(1.2e10, 4e6),
        name="attend_back",
    )(q, k, v, do, of, lse, segc)


def normal_cdf(value):
    power = jnp.exp(-0.5 * (value * value))
    size = jnp.abs(value)
    t = 1.0 / (1.0 + (0.3275911 * 0.7071067811865476) * size)
    poly = 1.061405429 * t - 1.453152027
    poly = poly * t + 1.421413741
    poly = poly * t - 0.284496736
    poly = poly * t + 0.254829592
    tail = (0.5 * poly) * (t * power)
    return jnp.where(value < 0.0, tail, 1.0 - tail), power * 0.3989422804014327


def row_mean(value):
    return jnp.mean(value, axis=-1, keepdims=True)


def fold(value):
    rows, width = value.shape
    return jnp.sum(value.reshape(rows // 8, 8, width), axis=0)


def slabs(count, rows, unroll, body):
    def step(i, carry):
        body(pl.ds(pl.multiple_of(i * rows, rows), rows))
        return carry

    lax.fori_loop(0, count // rows, step, 0, unroll=unroll)


def ffn_body(
    place_ref, at_ref, mx_ref, x_ref, cot_a_ref, cot_b_ref, wo_ref, bo_ref, g1_ref, s1_ref, wu_ref,
    bu_ref, wd_ref, bd_ref, g2_ref, s2_ref,
    act_own_ref, act_far_ref, res_ref, cg_ref, keep_ref, send_ref, small_ref,
    slope, active, up_grad, grouped, low_grad, hid_grad, joined, sums, up_sums, wide, norm, inverse,
):
    step = pl.program_id(0)
    block = at_ref.shape[0]
    blocks = active.shape[0] // block
    inner = at_ref.shape[1]
    width = x_ref.shape[1]
    part = width // GROUPS
    hidden = wu_ref.shape[2]
    chunk = 768
    rows, unroll = block, 1

    @pl.when(step == 0)
    def _():
        sums[...] = jnp.zeros_like(sums)
        up_sums[...] = jnp.zeros_like(up_sums)

    @pl.when(step < blocks)
    def _():
        t0 = pl.multiple_of(step * block, block)
        now = pl.ds(t0, block)
        own = step < blocks // 2
        joined[now, 0:inner] = at_ref[...]
        joined[now, inner:] = mx_ref[...]
        wide[...] = mm(joined[now, :], wo_ref[...])

        def first(slab):
            resid = x_ref[slab, :].astype(f32) + (wide[slab, :] + bo_ref[...])
            center = resid - row_mean(resid)
            inv = lax.rsqrt(row_mean(center * center) + EPS)
            inverse[slab, :] = jnp.broadcast_to(inv, (rows, LANES))
            normed = center * inv
            norm[slab, :] = normed
            grouped[pl.ds(pl.multiple_of(t0 + slab.start, rows), rows), :] = (
                normed * g1_ref[...] + s1_ref[...]
            ).astype(bf16)

        slabs(block, rows, unroll, first)

        for g in range(GROUPS):
            mine = slice(g * part, (g + 1) * part)
            low = None
            for c in range(hidden // chunk):
                cols = slice(c * chunk, (c + 1) * chunk)
                up = mm(grouped[now, mine], wu_ref[g, :, cols]) + bu_ref[g : g + 1, cols]
                cdf, density = normal_cdf(up)
                act = (up * cdf).astype(bf16)
                at = slice(g * hidden + c * chunk, g * hidden + (c + 1) * chunk)
                active[now, at] = act
                slope[:, at] = cdf + up * density
                add = mm(act, wd_ref[g, cols, :])
                low = add if low is None else low + add
            wide[:, mine] = low + bd_ref[g : g + 1, :]

        def second(slab):
            here = pl.ds(pl.multiple_of(t0 + slab.start, rows), rows)
            resid = (norm[slab, :] * g1_ref[...] + s1_ref[...]) + wide[slab, :]
            center = resid - row_mean(resid)
            inv = lax.rsqrt(row_mean(center * center) + EPS)
            normed = center * inv
            result = (normed * g2_ref[...] + s2_ref[...]).astype(bf16)
            hid_grad[here, :] = result
            grad = jnp.where(own, cot_a_ref[slab, :], cot_b_ref[slab, :]).astype(f32)
            sums[0:8, :] += fold(grad * normed)
            sums[8:16, :] += fold(grad)
            gs = grad * g2_ref[...]
            resid = inv * (gs - row_mean(gs) - normed * row_mean(gs * normed))
            wide[slab, :] = resid
            lg = resid.astype(bf16)
            low_grad[here, :] = lg
            sums[16:24, :] += fold(lg.astype(f32))

        slabs(block, rows, unroll, second)

        @pl.when(own)
        def _():
            act_own_ref[...] = hid_grad[now, :]

        @pl.when(jnp.logical_not(own))
        def _():
            act_far_ref[...] = hid_grad[now, :]

        for g in range(GROUPS):
            mine = slice(g * part, (g + 1) * part)
            back = None
            for c in range(hidden // chunk):
                cols = slice(c * chunk, (c + 1) * chunk)
                at = slice(g * hidden + c * chunk, g * hidden + (c + 1) * chunk)
                ag = mm_nt(low_grad[now, mine], wd_ref[g, cols, :])
                ug = (ag * slope[:, at]).astype(bf16)
                up_grad[now, at] = ug
                up_sums[:, at] += fold(ug.astype(f32))
                add = mm_nt(ug, wu_ref[g, :, cols])
                back = add if back is None else back + add
            wide[:, mine] += back

        def third(slab):
            here = pl.ds(pl.multiple_of(t0 + slab.start, rows), rows)
            grad = wide[slab, :]
            normed = norm[slab, :]
            inv = inverse[slab, 0:1]
            sums[24:32, :] += fold(grad * normed)
            sums[32:40, :] += fold(grad)
            gs = grad * g1_ref[...]
            resid = inv * (gs - row_mean(gs) - normed * row_mean(gs * normed))
            res_ref[slab, :] = resid
            hg = resid.astype(bf16)
            hid_grad[here, :] = hg
            sums[40:48, :] += fold(hg.astype(f32))

        slabs(block, rows, unroll, third)
        cg_ref[...] = mm_nt(hid_grad[now, :], wo_ref[...]).astype(bf16)

    per = hidden // 768

    def weight_grad(half, n):
        mine = slice(half * part, (half + 1) * part)
        if n < per:
            cols = slice(half * hidden + n * 768, half * hidden + (n + 1) * 768)
            return mm_tn(active[:, cols], low_grad[:, mine]).astype(bf16)
        if n < 2 * per:
            n -= per
            cols = slice(half * hidden + n * 768, half * hidden + (n + 1) * 768)
            value = mm_tn(grouped[:, mine], up_grad[:, cols]).astype(bf16)
        else:
            value = mm_tn(joined[:, mine], hid_grad[...]).astype(bf16)
        return jnp.concatenate([value[:, 0:part], value[:, part:]], axis=0)

    for n in range(2 * per + 1):

        @pl.when(step == blocks + n)
        def _():
            for half in range(2):
                store_half(
                    place_ref[1], half, keep_ref, send_ref, slice(None), weight_grad(half, n)
                )

    @pl.when(step == blocks)
    def _():
        across = width // 384
        small_ref[...] = jnp.zeros_like(small_ref)
        for n in range(6):
            line = jnp.sum(sums[8 * n : 8 * n + 8, :], axis=0, keepdims=True)
            for c in range(across):
                small_ref[across * n + c : across * n + c + 1, :] = line[:, c * 384 : (c + 1) * 384]
        line = jnp.sum(up_sums[...], axis=0, keepdims=True)
        for c in range(GROUPS * hidden // 384):
            at = 6 * across + c
            small_ref[at : at + 1, :] = line[:, c * 384 : (c + 1) * 384]


def store_half(core, half, keep_ref, send_ref, rows, value):
    @pl.when(core == half)
    def _():
        keep_ref[rows, :] = value

    @pl.when(core != half)
    def _():
        send_ref[rows, :] = value


def ffn(at, mx, x, cot, cot_far, place, wo, bo, g1, s1, wu, bu, wd, bd, g2, s2):
    length, width = x.shape
    inner = at.shape[1]
    block = length // 2
    blocks = length // block
    near = blocks // 2
    hidden = wu.shape[2]
    gsteps = 2 * (hidden // 768) + 1

    def turn(step, side_ref):
        s = jnp.minimum(step, blocks - 1)
        return (s + side_ref[0] * near) % blocks

    def tok(cols):
        return pl.BlockSpec((block, cols), lambda s, b: (turn(s, b), 0))

    def full(shape):
        return pl.BlockSpec(shape, lambda s, b: (0,) * len(shape), pipeline_mode=pl.Buffered(1))

    def near_map(s, b):
        return (jnp.minimum(s, near - 1), 0)

    def far_map(s, b):
        return (jnp.clip(s - near, 0, near - 1), 0)

    def cot_map(s, b):
        return (b[0], jnp.minimum(s, near - 1), 0)

    return pl.pallas_call(
        ffn_body,
        grid_spec=pltpu.PrefetchScalarGridSpec(
            num_scalar_prefetch=1,
            grid=(blocks + gsteps,),
            in_specs=[
                tok(inner), tok(inner), tok(width),
                pl.BlockSpec((None, block, width), cot_map),
                pl.BlockSpec((block, width), far_map),
                full(wo.shape), full(bo.shape), full(g1.shape), full(s1.shape), full(wu.shape),
                full(bu.shape), full(wd.shape), full(bd.shape), full(g2.shape), full(s2.shape),
            ],
            out_specs=(
                pl.BlockSpec((block, width), near_map),
                pl.BlockSpec((block, width), far_map),
                tok(width),
                tok(width),
                pl.BlockSpec((768, 384), lambda s, b: (jnp.maximum(s - blocks, 0), 0)),
                pl.BlockSpec((768, 384), lambda s, b: (jnp.maximum(s - blocks, 0), 0)),
                pl.BlockSpec((32, 384), lambda s, b: (0, 0)),
            ),
            scratch_shapes=[
                pltpu.VMEM((block, GROUPS * hidden), f32),
                pltpu.VMEM((length, GROUPS * hidden), bf16),
                pltpu.VMEM((length, GROUPS * hidden), bf16),
                pltpu.VMEM((length, width), bf16),
                pltpu.VMEM((length, width), bf16),
                pltpu.VMEM((length, width), bf16),
                pltpu.VMEM((length, width), bf16),
                pltpu.VMEM((48, width), f32),
                pltpu.VMEM((8, GROUPS * hidden), f32),
                pltpu.VMEM((block, width), f32),
                pltpu.VMEM((block, width), f32),
                pltpu.VMEM((block, LANES), f32),
            ],
        ),
        out_shape=(
            jax.ShapeDtypeStruct((length // 2, width), bf16),
            jax.ShapeDtypeStruct((length // 2, width), bf16),
            jax.ShapeDtypeStruct((length, width), f32),
            jax.ShapeDtypeStruct((length, width), bf16),
            jax.ShapeDtypeStruct((gsteps * 768, 384), bf16),
            jax.ShapeDtypeStruct((gsteps * 768, 384), bf16),
            jax.ShapeDtypeStruct((32, 384), f32),
        ),
        compiler_params=params(60),
        cost_estimate=cost(4e10, 3e7),
        name="ffn",
    )(place, at, mx, x, cot, cot_far, wo, bo, g1, s1, wu, bu, wd, bd, g2, s2)


def conv_back_body(
    q_ref, kc_ref, cv_ref, probs_ref, cg_ref, maskr_ref, w_ref, kw_ref, gather_ref,
    qc_ref, dg_ref, kcg, kwg_ref, small_ref,
    pad, prod, taps, kvg, sums,
):
    length, inner = q_ref.shape
    block, rows = 256, 32
    clear_pads(pad, length)

    @pl.loop(0, length // block)
    def _(i):
        t0 = pl.multiple_of(i * block, block)
        pad[pl.ds(pl.multiple_of(t0 + PAD, 16), block), :] = cv_ref[pl.ds(t0, block), :].astype(f32)

    tap_grads = []
    for b in range(length // block):

        @pl.loop(0, block // rows)
        def _(i):
            r0 = pl.multiple_of(i * rows, rows)
            t0 = pl.multiple_of(b * block + r0, rows)
            for c in range(inner // LANES):
                cols = slice(c * LANES, (c + 1) * LANES)
                win = window(pad, t0, rows, cols)
                mg = cg_ref[pl.ds(t0, rows), inner + c * LANES : inner + (c + 1) * LANES].astype(f32)
                for j in range(KERNEL):
                    prod[pl.ds(r0, rows), j * inner + c * LANES : j * inner + (c + 1) * LANES] = (
                        mg * moved(win, j - HALF, rows)
                    ).astype(bf16)

        tap_grads.append(jnp.transpose(mm(prod[...], gather_ref[...])))
    tap_grad = jnp.concatenate(tap_grads, axis=1)
    probs = [probs_ref[8 * j : 8 * j + 8, :] for j in range(KERNEL)]
    grads = [tap_grad[8 * j : 8 * j + 8, :] * maskr_ref[j : j + 1, :] for j in range(KERNEL)]
    dot = probs[0] * grads[0]
    for j in range(1, KERNEL):
        dot = dot + probs[j] * grads[j]
    rest = jnp.zeros((LANES - 8 * KERNEL, length), f32)
    logit = [(probs[j] * (grads[j] - dot)).astype(bf16).astype(f32) for j in range(KERNEL)]
    logit = jnp.concatenate(logit + [rest], axis=0)
    small_ref[...] = jnp.zeros_like(small_ref)
    for b in range(length // LANES):
        taps[b * LANES : (b + 1) * LANES, :] = jnp.transpose(
            logit[:, b * LANES : (b + 1) * LANES]
        ).astype(bf16)
    small_ref[0:1, 0:LANES] = jnp.sum(taps[...].astype(f32), axis=0, keepdims=True)
    sums[...] = jnp.zeros_like(sums)

    @pl.loop(0, length // block)
    def _(i):
        now = pl.ds(pl.multiple_of(i * block, block), block)
        mix_grad = mm(taps[now, :], kw_ref[...])
        q = q_ref[now, :].astype(f32)
        kc = kc_ref[now, :].astype(f32)
        low = (mix_grad * q).astype(bf16)
        kcg[now, :] = low
        kvg[now, :] = (kc * q).astype(bf16)
        sums[...] += fold(low.astype(f32))
        qc_ref[now, :] = mix_grad * kc
        dg_ref[now, :] = mm_nt(low, w_ref[2])

    kwg_ref[...] = mm_tn(taps[...], kvg[...]).astype(bf16)
    small_ref[1:2, :] = jnp.sum(sums[...], axis=0, keepdims=True)


def conv_back(q, kc, cv, probs, cg, maskr, weights, kw, gather):
    length, inner = q.shape
    width = cg.shape[1]
    return pl.pallas_call(
        conv_back_body,
        out_shape=(
            jax.ShapeDtypeStruct((length, inner), f32),
            jax.ShapeDtypeStruct((length, width), f32),
            jax.ShapeDtypeStruct((length, inner), bf16),
            jax.ShapeDtypeStruct((LANES, inner), bf16),
            jax.ShapeDtypeStruct((8, inner), f32),
        ),
        scratch_shapes=[
            pltpu.VMEM((length + 2 * PAD, inner), f32),
            pltpu.VMEM((256, KERNEL * inner), bf16),
            pltpu.VMEM((length, LANES), bf16),
            pltpu.VMEM((length, inner), bf16),
            pltpu.VMEM((8, inner), f32),
        ],
        compiler_params=params(48),
        cost_estimate=cost(1.2e10, 1e7),
        name="conv_back",
    )(q, kc, cv, probs, cg, maskr, weights, kw, gather)


def conv_values_body(
    place_ref, x_ref, dl_ref, kcg_ref, probs_ref, cg_ref, maskr_ref, expand_ref,
    vg_ref, kept_ref, sent_ref, small_ref,
    pad, taps, spread,
):
    length, width = x_ref.shape
    inner = kcg_ref.shape[1]
    block = 256
    clear_pads(pad, length)

    @pl.loop(0, length // block)
    def _(i):
        t0 = pl.multiple_of(i * block, block)
        pad[pl.ds(pl.multiple_of(t0 + PAD, 16), block), :] = cg_ref[
            pl.ds(t0, block), inner:
        ].astype(f32)

    low_taps = []
    for j in range(KERNEL):
        back = KERNEL - 1 - j
        low = probs_ref[8 * back : 8 * back + 8, :].astype(bf16).astype(f32)
        low = low * maskr_ref[back : back + 1, :]
        shift = (HALF - j) % length
        low_taps.append(pltpu.roll(low, shift, 1) if shift else low)
    taps_in_rows(low_taps, taps, length)
    conv_taps(taps, pad, expand_ref, spread, vg_ref, length)
    total = jnp.zeros((8, inner), f32)
    for i in range(length // block):
        total = total + fold(vg_ref[i * block : (i + 1) * block, :].astype(f32))
    small_ref[...] = jnp.zeros_like(small_ref)
    small_ref[0:1, :] = jnp.sum(total, axis=0, keepdims=True)
    core = place_ref[1]
    rows = slice(0, width)
    store_half(core, 0, kept_ref, sent_ref, rows, mm_tn(dl_ref[...], kcg_ref[...]).astype(bf16))
    store_half(core, 1, kept_ref, sent_ref, rows, mm_tn(x_ref[...], vg_ref[...]).astype(bf16))


def conv_values(place, x, dl, kcg, probs, cg, maskr, expand):
    length, width = x.shape
    inner = kcg.shape[1]
    vm = pl.BlockSpec(memory_space=pltpu.VMEM)
    return pl.pallas_call(
        conv_values_body,
        in_specs=[pl.BlockSpec(memory_space=pltpu.SMEM)] + [vm] * 7,
        out_specs=(vm,) * 4,
        out_shape=(
            jax.ShapeDtypeStruct((length, inner), bf16),
            jax.ShapeDtypeStruct((width + LANES, inner), bf16),
            jax.ShapeDtypeStruct((width + LANES, inner), bf16),
            jax.ShapeDtypeStruct((8, inner), f32),
        ),
        scratch_shapes=[
            pltpu.VMEM((length + 2 * PAD, inner), f32),
            pltpu.VMEM((length, LANES), bf16),
            pltpu.VMEM((256, KERNEL * inner), f32),
        ],
        compiler_params=params(48),
        cost_estimate=cost(1.2e10, 1e7),
        name="conv_values",
    )(place, x, dl, kcg, probs, cg, maskr, expand)


def depth_back_body(
    place_ref, x_ref, dg_ref, maskc_ref, dw_ref, kwg_ref, sf_ref, sc_ref, sv_ref, sw_ref,
    kept_ref, sent_ref, dx_ref, keep_ref, send_ref, gpad, dkg,
):
    length, width = x_ref.shape
    block, rows = 256, 32
    clear_pads(gpad, length)
    dkg[...] = jnp.zeros_like(dkg)

    @pl.loop(0, length // block)
    def _(i):
        t0 = pl.multiple_of(i * block, block)
        gpad[pl.ds(pl.multiple_of(t0 + PAD, 16), block), :] = dg_ref[pl.ds(t0, block), :]

    @pl.loop(0, length // rows)
    def _(i):
        t0 = pl.multiple_of(i * rows, rows)
        mask = maskc_ref[pl.ds(t0, rows), :]
        masks = [jnp.broadcast_to(mask[:, j : j + 1], (rows, LANES)) for j in range(KERNEL)]
        for c in range(width // LANES):
            cols = slice(c * LANES, (c + 1) * LANES)
            win = window(gpad, t0, rows, cols)
            x = x_ref[pl.ds(t0, rows), cols].astype(f32)
            total = jnp.zeros((rows, LANES), f32)
            for j in range(KERNEL):
                back = KERNEL - 1 - j
                part = moved(win, j - HALF, rows) * masks[j]
                total = total + dw_ref[back : back + 1, cols] * part
                dkg[8 * back : 8 * back + 8, cols] += fold(part * x)
            dx_ref[pl.ds(t0, rows), cols] = total

    across = width // 384
    lines = []
    for j in range(KERNEL):
        line = jnp.sum(dkg[8 * j : 8 * j + 8, :], axis=0, keepdims=True)
        lines += [line[:, c * 384 : (c + 1) * 384] for c in range(across)]
    smalls = [sf_ref[...], sc_ref[...], sv_ref[...], sw_ref[...]] + lines
    used = sum(v.shape[0] for v in smalls)
    smalls = jnp.concatenate(smalls + [jnp.zeros((LANES - used, 384), f32)], axis=0)
    core = place_ref[1]
    keep_ref[0:width, :] = kept_ref[0:width, :]
    send_ref[0:width, :] = sent_ref[0:width, :]
    rows = slice(width, width + LANES)
    store_half(core, 0, keep_ref, send_ref, rows, kwg_ref[...])
    store_half(core, 1, keep_ref, send_ref, rows, smalls.astype(bf16))


def depth_back(place, x, dg, maskc, dw, kwg, sf, sc, sv, sw, kept, sent):
    length, width = x.shape
    vm = pl.BlockSpec(memory_space=pltpu.VMEM)
    return pl.pallas_call(
        depth_back_body,
        in_specs=[pl.BlockSpec(memory_space=pltpu.SMEM)] + [vm] * 11,
        out_specs=(vm,) * 3,
        out_shape=(
            jax.ShapeDtypeStruct((length, width), f32),
            jax.ShapeDtypeStruct(kept.shape, bf16),
            jax.ShapeDtypeStruct(kept.shape, bf16),
        ),
        scratch_shapes=[
            pltpu.VMEM((length + 2 * PAD, width), f32),
            pltpu.VMEM((8 * KERNEL, width), f32),
        ],
        compiler_params=params(40),
        cost_estimate=cost(1.2e10, 1e7),
        name="depth_back",
    )(place, x, dg, maskc, dw, kwg, sf, sc, sv, sw, kept, sent)


def wgrad_body(
    place_ref, x_ref, *refs
):
    pairs = 3
    dqs, dks, dvs = refs[0:pairs], refs[pairs : 2 * pairs], refs[2 * pairs : 3 * pairs]
    qc_ref, keep_ref, send_ref, dqkv_ref, small_ref = refs[3 * pairs :]
    length, width = x_ref.shape
    inner = qc_ref.shape[1]
    for p in range(pairs):
        cols = slice(p * LANES, (p + 1) * LANES)
        dqkv_ref[:, cols] = (dqs[p][...] + qc_ref[:, cols]).astype(bf16)
        dqkv_ref[:, inner + p * LANES : inner + (p + 1) * LANES] = dks[p][...]
        dqkv_ref[:, 2 * inner + p * LANES : 2 * inner + (p + 1) * LANES] = dvs[p][...]
    core = place_ref[1]
    step = 384
    count = 3 * (width // step)
    for n in range(count):
        which, piece = divmod(n, width // step)
        value = mm_tn(
            x_ref[:, piece * step : (piece + 1) * step],
            dqkv_ref[:, which * inner : (which + 1) * inner],
        ).astype(bf16)
        half, at = divmod(n, count // 2)
        store_half(core, half, keep_ref, send_ref, slice(at * step, (at + 1) * step), value)
    total = jnp.zeros((8, 3 * inner), f32)
    for i in range(length // 256):
        total = total + fold(dqkv_ref[i * 256 : (i + 1) * 256, :].astype(f32))
    line = jnp.sum(total, axis=0, keepdims=True)
    small_ref[...] = jnp.zeros_like(small_ref)
    for which in range(3):
        small_ref[which : which + 1, :] = line[:, which * inner : (which + 1) * inner]


def wgrad(place, x, dqs, dks, dvs, qc):
    length, width = x.shape
    inner = qc.shape[1]
    rows = 3 * width // 2
    vm = pl.BlockSpec(memory_space=pltpu.VMEM)
    return pl.pallas_call(
        wgrad_body,
        in_specs=[pl.BlockSpec(memory_space=pltpu.SMEM)] + [vm] * 11,
        out_specs=(vm,) * 4,
        out_shape=(
            jax.ShapeDtypeStruct((rows, inner), bf16),
            jax.ShapeDtypeStruct((rows, inner), bf16),
            jax.ShapeDtypeStruct((length, 3 * inner), bf16),
            jax.ShapeDtypeStruct((8, inner), f32),
        ),
        compiler_params=params(40),
        cost_estimate=cost(6e9, 1e7),
        name="wgrad",
    )(place, x, *dqs, *dks, *dvs, qc)


def xgrad_body(place_ref, dqkv_ref, vg_ref, dxd_ref, res_ref, wq_ref, w_ref, out_ref):
    inner = vg_ref.shape[1]
    total = res_ref[...] + dxd_ref[...]
    total = total + mm_nt(vg_ref[...], w_ref[3])
    total = total + mm_nt(dqkv_ref[:, 0:inner], wq_ref[...])
    total = total + mm_nt(dqkv_ref[:, inner : 2 * inner], w_ref[0])
    total = total + mm_nt(dqkv_ref[:, 2 * inner :], w_ref[1])
    out_ref[...] = total.astype(out_ref.dtype)


def xgrad(place, far, dqkv, vg, dxd, res, wq, weights):
    length, width = res.shape
    inner = vg.shape[1]
    block = 256
    near = length // 2 // block

    def tok(cols):
        def index(s, b):
            half = 1 - b[0] if far else b[0]
            return (half * near + s, 0)

        return pl.BlockSpec((block, cols), index)

    def full(shape):
        return pl.BlockSpec(shape, lambda s, b: (0,) * len(shape), pipeline_mode=pl.Buffered(1))

    return pl.pallas_call(
        xgrad_body,
        grid_spec=pltpu.PrefetchScalarGridSpec(
            num_scalar_prefetch=1,
            grid=(near,),
            in_specs=[
                tok(3 * inner), tok(inner), tok(width), tok(width), full(wq.shape),
                full(weights.shape),
            ],
            out_specs=pl.BlockSpec((block, width), lambda s, b: (s, 0)),
        ),
        out_shape=jax.ShapeDtypeStruct((length // 2, width), bf16 if far else f32),
        compiler_params=params(40),
        cost_estimate=cost(3e9, 8e6),
        name="xgrad_far" if far else "xgrad_own",
    )(place, dqkv, vg, dxd, res, wq, weights)


def unpack_ffn_body(place_ref, mine_ref, got_ref, down_ref, up_ref, out_ref):
    step = pl.program_id(0)
    per = pl.num_programs(0) // 2
    own = step // per == place_ref[1]
    value = jnp.where(own, mine_ref[...], got_ref[...]).astype(f32)
    n = step % per
    half = value.shape[0] // 2

    @pl.when(n < per // 2)
    def _():
        down_ref[...] = value

    @pl.when((n >= per // 2) & (n < per - 1))
    def _():
        up_ref[:, 0:384] = value[:half]
        up_ref[:, 384:] = value[half:]

    @pl.when(n == per - 1)
    def _():
        out_ref[:, 0:384] = value[:half]
        out_ref[:, 384:] = value[half:]


def unpack_ffn(place, mine, got, hidden):
    rows, part = mine.shape
    per = rows // 768
    each = per // 2

    def source(half_of):
        def index(s, b):
            half = b[1] if half_of else 1 - b[1]
            return (jnp.clip(s - per * half, 0, per - 1), 0)

        return pl.BlockSpec((768, part), index)

    return pl.pallas_call(
        unpack_ffn_body,
        grid_spec=pltpu.PrefetchScalarGridSpec(
            num_scalar_prefetch=1,
            grid=(2 * per,),
            in_specs=[source(True), source(False)],
            out_specs=(
                pl.BlockSpec(
                    (768, part), lambda s, b: (each * (s // per) + jnp.minimum(s % per, each - 1), 0)
                ),
                pl.BlockSpec(
                    (None, part, 768),
                    lambda s, b: (s // per, 0, jnp.clip(s % per - each, 0, each - 1)),
                ),
                pl.BlockSpec((part, 2 * part), lambda s, b: (s // per, 0)),
            ),
        ),
        out_shape=(
            jax.ShapeDtypeStruct((GROUPS * hidden, part), f32),
            jax.ShapeDtypeStruct((GROUPS, part, hidden), f32),
            jax.ShapeDtypeStruct((2 * part, 2 * part), f32),
        ),
        compiler_params=params(32),
        cost_estimate=cost(1e6, 2e7),
        name="unpack_ffn",
    )(place, mine, got)


def unpack_mixers_body(place_ref, cm_ref, cg_ref, am_ref, ag_ref, query_ref, stack_ref):
    width = query_ref.shape[0]
    half = width // 2
    for core in range(2):

        @pl.when(place_ref[1] == core)
        def _():
            conv = (cm_ref, cg_ref) if core == 0 else (cg_ref, cm_ref)
            rest = (am_ref, ag_ref) if core == 0 else (ag_ref, am_ref)
            query_ref[...] = rest[0][0:width, :].astype(f32)

            @pl.when(place_ref[0] == 0)
            def _():
                stack_ref[0, 0:half, :] = rest[0][width:, :].astype(f32)
                stack_ref[0, half:, :] = rest[1][0:half, :].astype(f32)
                stack_ref[1] = rest[1][half:, :].astype(f32)

            @pl.when(place_ref[0] != 0)
            def _():
                stack_ref[0] = conv[0][0:width, :].astype(f32)
                stack_ref[1] = conv[1][0:width, :].astype(f32)


def unpack_mixers(place, conv_mine, conv_got, mine, got):
    inner = conv_mine.shape[1]
    width = mine.shape[0] * 2 // 3
    vm = pl.BlockSpec(memory_space=pltpu.VMEM)
    return pl.pallas_call(
        unpack_mixers_body,
        in_specs=[pl.BlockSpec(memory_space=pltpu.SMEM)] + [vm] * 4,
        out_specs=(vm, vm),
        out_shape=(
            jax.ShapeDtypeStruct((width, inner), f32),
            jax.ShapeDtypeStruct((2, width, inner), f32),
        ),
        compiler_params=params(32),
        cost_estimate=cost(1e6, 8e6),
        name="unpack_mixers",
    )(place, conv_mine, conv_got, mine, got)


AXES = ("branch", "dp")


def joint(value, count, masks):
    return lax.ppermute(value, AXES, [(i, i ^ masks[i & 1]) for i in range(count)])


class Sum:
    def __init__(self, kept, sent, index, count, plan):
        self.index, self.count = index, count
        self.plan = [[(1, 1)]] + plan
        self.depth = 0
        self.value, self.sent = kept, [sent]
        self.got = None
        self.down = True

    def hops(self):
        first = self.plan[self.depth]
        if len(first) == 1:
            return first
        (a, b), (c, d) = first
        return [(a, b), (c, d), (a ^ c, b ^ d)]

    def spot(self):
        at = jnp.int32(0)
        for n, masks in enumerate(self.plan[self.depth]):
            mask = jnp.where(self.index % 2 == 0, masks[0], masks[1])
            at = at + jnp.where((self.index & mask) != 0, 1 << n, 0)
        return at

    def start(self):
        sent = self.sent if self.down else [self.value] * 3
        self.got = [joint(v, self.count, masks) for v, masks in zip(sent, self.hops())]

    def finish(self):
        got, self.got = self.got, None
        if self.down:
            total = [self.value] + got
            if self.depth + 1 == len(self.plan):
                self.value, self.sent = added(total), []
                self.down = False
                return
            self.depth += 1
            spot = self.spot()
            ways = len(self.hops()) + 1
            rows = self.value.shape[0] // ways
            pieces = []
            for k in range(ways):
                at = (spot ^ k) * rows
                pieces.append(added([lax.dynamic_slice_in_dim(v, at, rows, 0) for v in total]))
            self.value, self.sent = pieces[0], pieces[1:]
            return
        spot = self.spot()
        rows = self.value.shape[0]
        if len(got) == 1:
            first = spot == 0
            self.value = jnp.concatenate(
                [jnp.where(first, self.value, got[0]), jnp.where(first, got[0], self.value)]
            )
        else:
            whole = jnp.zeros((4 * rows, self.value.shape[1]), self.value.dtype)
            for k, piece in enumerate([self.value] + got):
                whole = lax.dynamic_update_slice_in_dim(whole, piece, (spot ^ k) * rows, 0)
            self.value = whole
        self.depth -= 1

    @property
    def last(self):
        return not self.down and self.depth == 0

    def live(self):
        return [self.value] + self.sent

    def put(self, values):
        self.value, self.sent = values[0], list(values[1:])

    def halves(self):
        while True:
            if self.got is None:
                self.start()
            if self.last:
                return self.value, self.got[0]
            self.finish()


def added(values):
    total = values[0].astype(f32)
    for v in values[1:]:
        total = total + v.astype(f32)
    return total.astype(bf16)


def tick(finish, start, held=()):
    for chain in finish:
        if chain.got is not None and not chain.last:
            chain.finish()
    chains = [chain for chain in dict.fromkeys(list(finish) + list(start)) if chain.got is None]
    flat = [v for chain in chains for v in chain.live()]
    tied = lax.optimization_barrier(tuple(flat) + tuple(held))
    at = 0
    for chain in chains:
        n = len(chain.live())
        chain.put(tied[at : at + n])
        at += n
    for chain in start:
        if chain.got is None:
            chain.start()
    return tied[at:]


def local(sizes):
    branches, ranks = sizes["branch"], sizes["dp"]
    count = branches * ranks
    bits = []
    while (2 << len(bits)) < ranks:
        bits.append(2 << len(bits))
    along = ranks
    far = [[(b, b) for b in bits[n : n + 2]] for n in range(1, len(bits), 2)]
    pairs = [[(bits[0], along)], [(along, bits[0])]] + far
    fours = [[(along, along), (bits[0], bits[0])]] + far

    def run(
        inputs, segments, query_weight, query_bias, branch_weights, value_bias, depthwise,
        point_bias, kernel_weight, kernel_bias, conv_bias, output_weight, output_bias, first_gain,
        first_shift, up_weight, up_bias, down_weight, down_bias, second_gain, second_shift,
        cotangent,
    ):
        seqs, length, width = inputs.shape
        inner = query_weight.shape[1]
        hidden = up_weight.shape[2]
        part = width // GROUPS
        side = lax.axis_index("branch").astype(jnp.int32)
        rank = lax.axis_index("dp").astype(jnp.int32)
        core = rank % 2
        index = side * ranks + rank
        place = jnp.stack([side, core])
        first = side == 0

        def across(value):
            return joint(value, count, (along, along))

        got = across(lax.dynamic_index_in_dim(branch_weights[0], core, 0, keepdims=False))
        x = lax.dynamic_index_in_dim(inputs, side, 0, keepdims=False)
        seg = lax.dynamic_index_in_dim(segments, side, 0, keepdims=False)

        spots = jnp.arange(length)
        around = spots[None, :] + (jnp.arange(KERNEL) - HALF)[:, None]
        inside = (around >= 0) & (around < length)
        padded = jnp.pad(seg, (HALF, HALF), constant_values=-1)
        near = jnp.stack([lax.slice_in_dim(padded, j, j + length) for j in range(KERNEL)])
        maskr = ((near == seg[None, :]) & inside).astype(f32)
        maskr = jnp.pad(maskr, ((0, 16 - KERNEL), (0, 0)))
        maskc = maskr.T
        segc = jnp.broadcast_to(seg[:, None], (length, LANES))

        kw = kernel_weight.reshape(inner, HEADS, KERNEL).transpose(2, 1, 0)
        kw = jnp.pad(kw, ((0, 0), (0, 8 - HEADS), (0, 0))).reshape(8 * KERNEL, inner)
        kw_wide = jnp.pad(kw, ((0, LANES - 8 * KERNEL), (0, 0)))
        kb = kernel_bias.reshape(HEADS, KERNEL).T
        kb = jnp.pad(kb, ((0, 0), (0, 8 - HEADS))).reshape(8 * KERNEL, 1)
        kb = jnp.broadcast_to(kb, (8 * KERNEL, LANES))

        lane = jnp.arange(KERNEL * inner)
        slot = (lane // inner) * 8 + (lane % inner) // HEAD
        expand = (jnp.arange(LANES)[:, None] == slot[None, :]).astype(bf16)
        gather = (slot[:, None] == jnp.arange(LANES)[None, :]).astype(bf16)

        q, dl = front(x, maskc, query_weight, query_bias[None], depthwise)
        cot_sent = lax.dynamic_index_in_dim(cotangent, 1 - side, 0, keepdims=False)
        got, cot_sent = lax.optimization_barrier((got, cot_sent))
        got2 = joint(got, count, (1, 1))
        cot_far = across(cot_sent)
        k, v, kc, cv, probs, mixed, weights = mixers(
            place, x, q, dl, maskr, branch_weights[0], got, got2, value_bias[None],
            point_bias[None], conv_bias[None], kw, kb, expand,
        )
        attended, attended_f, lse = attend(q, k, v, segc)

        act_own, act_far, resid, cg, keep, send, small_f = ffn(
            attended, mixed, x, cotangent, cot_far, place, output_weight, output_bias[None],
            first_gain[None], first_shift[None], up_weight, up_bias, down_weight,
            down_bias, second_gain[None], second_shift[None],
        )
        ffn_sum = Sum(keep, send, index, count, pairs)
        (cg,) = tick([], [ffn_sum], [cg])
        act_got = across(act_far)
        qc, dg, kcg, kwg, small_c = conv_back(
            q, kc, cv, probs, cg, maskr, weights, kw_wide, gather
        )
        cg, qc = tick([ffn_sum], [ffn_sum], [cg, qc])
        back = []
        for pair in range(inner // LANES):
            out = attend_back(pair, q, k, v, cg, attended_f, lse, segc)
            if pair == 0:
                cg, *out = lax.optimization_barrier((cg, *out))
            else:
                cg, act_got, *out = tick([ffn_sum], [ffn_sum], [cg, act_got, *out])
            back.append(tuple(out))
        dqs, dks, dvs = zip(*back)
        keep, send, dqkv, small_w = wgrad(place, x, dqs, dks, dvs, qc)
        last_sum = Sum(keep, send, index, count, fours)
        (kcg,) = tick([], [last_sum], [kcg])
        vg, keep, send, small_v = conv_values(place, x, dl, kcg, probs, cg, maskr, expand)
        dg, vg = tick([last_sum], [last_sum], [dg, vg])
        dxd, keep, send = depth_back(
            place, x, dg, maskc, depthwise, kwg, small_f, small_c, small_v, small_w, keep, send
        )
        conv_sum = Sum(keep, send, index, count, fours)
        (dxd,) = tick([ffn_sum], [ffn_sum, conv_sum], [dxd])
        far = xgrad(place, True, dqkv, vg, dxd, resid, query_weight, weights)
        dxd, far = lax.optimization_barrier((dxd, far))
        grad_got = across(far)
        own = xgrad(place, False, dqkv, vg, dxd, resid, query_weight, weights)
        (own,) = tick([last_sum, conv_sum], [last_sum, conv_sum], [own])
        activations = jnp.stack(
            [jnp.where(first, act_own, act_got), jnp.where(first, act_got, act_own)]
        )
        grad_got, activations = tick([last_sum], [last_sum], [grad_got, activations])
        grad_far = grad_got.astype(f32)
        input_grad = jnp.stack([jnp.where(first, own, grad_far), jnp.where(first, grad_far, own)])
        (input_grad,) = tick([ffn_sum, conv_sum], [ffn_sum, conv_sum], [input_grad])
        tick([last_sum, conv_sum], [last_sum, conv_sum])
        tick([ffn_sum, conv_sum], [ffn_sum, conv_sum])
        tick([last_sum], [last_sum])
        tick([ffn_sum, conv_sum], [ffn_sum, conv_sum])

        last_halves = last_sum.halves()
        conv_halves = conv_sum.halves()
        small_mine, small_got = (v[width:] for v in conv_halves)
        query_grad, stack = unpack_mixers(place, *conv_halves, *last_halves)
        ffn_halves = ffn_sum.halves()
        down, up, out = unpack_ffn(place, *ffn_halves, hidden)
        down = down.reshape(GROUPS, hidden, part)

        even = core == 0
        kernel_grad = jnp.where(even, small_mine, small_got).astype(f32)
        small = jnp.where(even, small_got, small_mine).astype(f32)
        kernel_grad = kernel_grad[: 8 * KERNEL].reshape(KERNEL, 8, inner)[:, :HEADS]
        kernel_grad = kernel_grad.transpose(2, 1, 0).reshape(inner, HEADS * KERNEL)
        lines = width // inner
        smalls = small[: 6 * lines].reshape(6, width)
        up_bias_grad = small[6 * lines : 6 * lines + GROUPS * hidden // inner]
        up_bias_grad = up_bias_grad.reshape(GROUPS, hidden)
        kb_grad, point_bias_grad, conv_bias_grad = small[32], small[33], small[40]
        query_bias_grad, value_bias_grad = small[48], small[50]
        depth_grad = small[56 : 56 + KERNEL * lines].reshape(KERNEL, width)
        kb_grad = kb_grad[: 8 * KERNEL].reshape(KERNEL, 8)[:, :HEADS].T.reshape(-1)

        return (
            activations, input_grad, query_grad, query_bias_grad, stack[None],
            value_bias_grad, depth_grad, point_bias_grad, kernel_grad, kb_grad,
            conv_bias_grad, out, smalls[5], smalls[3], smalls[4], up, up_bias_grad, down,
            smalls[2].reshape(GROUPS, part), smalls[0], smalls[1],
        )

    return run


def solution(mesh):
    whole = P()
    tokens = P("dp", "branch", None)
    stack = P("branch", None, None, None)
    placed = (
        (P("dp", None, None), P("dp", None), whole, whole, stack) + (whole,) * 16 + (tokens,)
    )
    return jax.shard_map(
        local(dict(mesh.shape)),
        mesh=mesh,
        in_specs=placed,
        out_specs=(tokens, tokens, whole, whole, stack) + (whole,) * 16,
        check_vma=False,
    )
```

time: 934 us -> 339 us (0.36)
  matrix products: 311 us -> 0 us
  waiting for transfers between devices: 262 us -> 55 us
  Pallas kernels: 0 us -> 181 us
  local copies, waits for them, and re-layouts: 141 us -> 29.4 us
  other arithmetic: 109 us -> 14.5 us
  blocking collectives: 68.8 us -> 0 us
  starting transfers between devices: 17.5 us -> 50.7 us
  between operations: 15.1 us -> 2.33 us
    dot_general x34 -> x0, matrix products: 311 us -> none  [the longest x4 56.3 us: attention_scores(): jnp.einsum('sqhe,skhe->shqk', query_block, key_heads, preferred_element_t...]
    psum x2 -> x0, waiting for transfers between devices: 225 us -> none  [the longest x1 225 us: local(): lax.psum((query_weight_grad, query_bias_grad, value_bias_grad, depthwise_...]
    pallas_call x0 -> x15, Pallas kernels: none -> 181 us  [the longest x1 56.8 us: ffn(): pl.pallas_call(ffn_body, grid_spec=pltpu.PrefetchScalarGridSpec(num_scala...]
    psum x1 -> x0, blocking collectives: 68.8 us -> none  [local(): lax.psum((query_weight_grad, query_bias_grad, value_bias_grad, depthwise_...]
    ppermute x0 -> x45, waiting for transfers between devices: none -> 55 us  [joint(): lax.ppermute(value, AXES, [(i, i ^ masks[i & 1]) for i in range(count)])]
    ppermute x0 -> x45, starting transfers between devices: none -> 50.7 us  [joint(): lax.ppermute(value, AXES, [(i, i ^ masks[i & 1]) for i in range(count)])]
    reduce_sum x11 -> x0, other arithmetic: 49 us -> none  [the longest x2 26.5 us: one_block(): summed = jnp.sum(powers, axis=-1, keepdims=True)]
    convert_element_type x5 -> x12, other arithmetic: 54.3 us -> 6.86 us  [the longest x10 4.26 us: added(): return total.astype(bf16)]
  transfers between devices with their start and end apart: 6 -> 45, of which waited for: 4 -> 16; matrix products, arithmetic and copies ran while one was open for 5% -> 8% of each run, Pallas kernels for 0% -> 30%
where the time goes in v1:
time: 339 us; the launch traced here: 333 us
  Pallas kernels  181 us (53%)
  waiting for transfers between devices  55 us (16%)
  starting transfers between devices  50.7 us (15%)
  local copies, waits for them, and re-layouts  29.4 us (9%)
  other arithmetic  14.5 us (4%)
    pallas_call x1, Pallas kernels, ffn(): pl.pallas_call(ffn_body, grid_spec=pltpu.PrefetchScalarGridSpec(num_scala...  56.8 us
    ppermute x45, waiting for transfers between devices, joint(): lax.ppermute(value, AXES, [(i, i ^ masks[i & 1]) for i in range(count)])  55 us
    ppermute x45, starting transfers between devices, joint(): lax.ppermute(value, AXES, [(i, i ^ masks[i & 1]) for i in range(count)])  50.7 us
    pallas_call x3, Pallas kernels, attend_back(): pl.pallas_call(attend_back_body, grid=(1,), in_specs=[pair] * 6 + [fixed]...  34.3 us
    pallas_call x1, Pallas kernels, attend(): pl.pallas_call(attend_body, grid=(inner // LANES,), in_specs=[pair, pair,...  15.9 us
    pallas_call x1, Pallas kernels, mixers(): pl.pallas_call(mixers_body, in_specs=[pl.BlockSpec(memory_space=pltpu.SME...  13.5 us
    unnamed x124, local copies, waits for them, and re-layouts  12.2 us
    pallas_call x1, Pallas kernels, unpack_ffn(): pl.pallas_call(unpack_ffn_body, grid_spec=pltpu.PrefetchScalarGridSpec(nu...  12.1 us
  transfers between devices with their start and end apart: 45, of which 16 were waited for; matrix products, arithmetic and copies ran while one was open for 8% of the time, Pallas kernels for 30%

profile of v1, /device:TPU:0, one launch (start us, length us, event | category | flops | bytes accessed | tf_op | source)
XLA Modules:
  0.0 333.3 jit_solution(18187793412961355697)
XLA Ops:
  2.8 2.9 collective-permute-start
  10.3 7.0 %front.1 = (bf16[1024,384]{1,0:T(8,128)(2,1)S(1)}, bf16[1024,768]{1,0:T(8,128)(2,1)S(1)}) custom-call(bf16[1024,768]{1,0:T(8,128)(2,1)S(1)} %copy-done.8, f32[1024,16]{1,0:T(8,128)S(1)} %bitcast.44, bf16[768,384]{1,0:T(8,128)(2,1)S(1)} %copy-done.6, f32[1,384]{1,0:T(1,128)S(1)} %broadcast_in_dim.65.bq_ref, f32[9,768]{1,0:T(8,128)S(1)} %copy-done.16), custom_call_target="tpu_custom_call" | custom-call | flops 20000000000 | bytes 8000000 | tf_op jit(solution)/shard_map/front/pallas_call | solution.py:96
  25.5 13.5 %mixers.1 = (bf16[1024,384]{1,0:T(8,128)(2,1)S(1)}, bf16[1024,384]{1,0:T(8,128)(2,1)S(1)}, bf16[1024,384]{1,0:T(8,128)(2,1)S(1)}, bf16[1024,384]{1,0:T(8,128)(2,...) custom-call(s32[2]{0:T(128)S(1)} %pad_add_fusion.place_ref, ...), custom_call_target="tpu_custom_call" | custom-call | flops 20000000000 | bytes 10000000 | tf_op jit(solution)/shard_map/mixers/pallas_call | solution.py:195
  40.9 15.9 %attend.1 = (bf16[1024,384]{1,0:T(8,128)(2,1)S(1)}, f32[1024,384]{1,0:T(8,128)S(1)}, f32[1024,384]{1,0:T(8,128)S(1)}) custom-call(bf16[1024,384]{1,0:T(8,128)(2,1)S(1)} %copy-done.24, bf16[1024,384]{1,0:T(8,128)(2,1)S(1)} %get-tuple-element.141.k_ref, bf16[1024,384]{1,0:T(8,128)(2,1)S(1)} %get-tuple-element.142.v_ref, s32[1024,128]{1,0:T(8,128)S(1)} %broadcast_in_dim.71.segc_ref), custom_call_target="tpu_custom_call" | custom-call | flops 20000000000 | bytes 10000000 | tf_op jit(solution)/shard_map/attend/pallas_call | solution.py:263
  61.1 56.8 %ffn.1 = (bf16[512,768]{1,0:T(8,128)(2,1)}, bf16[512,768]{1,0:T(8,128)(2,1)}, f32[1024,768]{1,0:T(8,128)}, bf16[1024,768]{1,0:T(8,128)(2,1)}, bf16[3840,384]{1,0...) custom-call(s32[2]{0:T(128)} %copy-done.14, bf16[1024,384]{1,0:T(8,128)(2,1)} %copy-done.42, ...), custom_call_target="tpu_custom_call" | custom-call | flops 40000000000 | bytes 30000000 | tf_op jit(solution)/shard_map/ffn/pallas_call | solution.py:601
  120.8 10.9 %conv_back.1 = (f32[1024,384]{1,0:T(8,128)S(1)}, f32[1024,768]{1,0:T(8,128)}, bf16[1024,384]{1,0:T(8,128)(2,1)S(1)}, bf16[128,384]{1,0:T(8,128)(2,1)S(1)}, f32[8,384]{1,0:T(8,128)S(1)}) custom-call(bf16[1024,384]{1,0:T(8,128)(2,1)S(1)} %copy-done.25, bf16[1024,384]{1,0:T(8,128)(2,1)S(1)} %copy-done.27, bf16[1024,384]{1,0:T(8,128)(2,1)S(1)} %copy-done.29, ...), custom_call_target="tpu_custom_call" | custom-call | flops 12000000000 | bytes 10000000 | tf_op jit(solution)/shard_map/conv_back/pallas_call | solution.py:720
  131.8 2.9 add_convert_fusion
  136.3 11.4 %attend_back.3 = (f32[1024,128]{1,0:T(8,128)S(1)}, bf16[1024,128]{1,0:T(8,128)(2,1)S(1)}, bf16[1024,128]{1,0:T(8,128)(2,1)S(1)}) custom-call(bf16[1024,384]{1,0:T(8,128)(2,1)S(1)} %copy-done.25, bf16[1024,384]{1,0:T(8,128)(2,1)S(1)} %copy-done.33, bf16[1024,384]{1,0:T(8,128)(2,1)S(1)} %copy-done.35, bf16[1024,768]{1,0:T(8,128)(2,1)S(1)} %copy-done.19, ...), custom_call_target="tpu_custom_call" | custom-call | flops 12000000000 | bytes 4000000 | tf_op jit(solution)/shard_map/attend_back/pallas_call | solution.py:357
  147.6 11.6 %attend_back.4 = (f32[1024,128]{1,0:T(8,128)S(1)}, bf16[1024,128]{1,0:T(8,128)(2,1)S(1)}, bf16[1024,128]{1,0:T(8,128)(2,1)S(1)}) custom-call(bf16[1024,384]{1,0:T(8,128)(2,1)S(1)} %copy-done.25, bf16[1024,384]{1,0:T(8,128)(2,1)S(1)} %copy-done.33, bf16[1024,384]{1,0:T(8,128)(2,1)S(1)} %copy-done.35, bf16[1024,768]{1,0:T(8,128)(2,1)S(1)} %copy-done.19, ...), custom_call_target="tpu_custom_call" | custom-call | flops 12000000000 | bytes 4000000 | tf_op jit(solution)/shard_map/attend_back/pallas_call | solution.py:357
  160.7 11.4 %attend_back.5 = (f32[1024,128]{1,0:T(8,128)S(1)}, bf16[1024,128]{1,0:T(8,128)(2,1)S(1)}, bf16[1024,128]{1,0:T(8,128)(2,1)S(1)}) custom-call(bf16[1024,384]{1,0:T(8,128)(2,1)S(1)} %copy-done.25, bf16[1024,384]{1,0:T(8,128)(2,1)S(1)} %copy-done.33, bf16[1024,384]{1,0:T(8,128)(2,1)S(1)} %copy-done.35, bf16[1024,768]{1,0:T(8,128)(2,1)S(1)} %copy-done.19, ...), custom_call_target="tpu_custom_call" | custom-call | flops 12000000000 | bytes 4000000 | tf_op jit(solution)/shard_map/attend_back/pallas_call | solution.py:357
  173.5 5.0 %wgrad.1 = (bf16[1152,384]{1,0:T(8,128)(2,1)S(1)}, bf16[1152,384]{1,0:T(8,128)(2,1)S(1)}, bf16[1024,1152]{1,0:T(8,128)(2,1)S(1)}, f32[8,384]{1,0:T(8,128)S(1)}) custom-call(s32[2]{0:T(128)S(1)} %copy-done.15, bf16[1024,768]{1,0:T(8,128)(2,1)S(1)} %copy-done.9, f32[1024,128]{1,0:T(8,128)S(1)} %get-tuple-element.163.refs_0_, ...), custom_call_target="tpu_custom_call" | custom-call | flops 6000000000 | bytes 10000000 | tf_op jit(solution)/shard_map/wgrad/pallas_call | solution.py:911
  178.6 3.7 %collective-permute-start.13 = (bf16[240,384]{1,0:T(8,128)(2,1)S(1)}, bf16[240,384]{1,0:T(8,128)(2,1)S(1)}, u32[]{:S(2)}, u32[]{:S(2)}) collective-permute-start(bf16[240,384]{1,0:T(8,128)(2,1)S(1)} %get-tuple-element.203), channel_id=1, source_target_pairs={{0,12},{1,13},{2,14},{3,15},{4,8},{5,9},{6,10},{7,11},{8,4},{9,5},... | collective-permute-start | bytes 552968 | tf_op jit(solution)/shard_map/ppermute | solution.py:1079
  183.1 9.2 %conv_values.1 = (bf16[1024,384]{1,0:T(8,128)(2,1)S(1)}, bf16[896,384]{1,0:T(8,128)(2,1)S(1)}, bf16[896,384]{1,0:T(8,128)(2,1)S(1)}, f32[8,384]{1,0:T(8,128)S(1)}) custom-call(s32[2]{0:T(128)S(1)} %copy-done.15, bf16[1024,768]{1,0:T(8,128)(2,1)S(1)} %copy-done.9, bf16[1024,768]{1,0:T(8,128)(2,1)} %copy-done.22, bf16[1024,384]{1,0:T(8,128)(2,1)S(1)} %copy-done.31, ...), custom_call_target="tpu_custom_call" | custom-call | flops 12000000000 | bytes 10000000 | tf_op jit(solution)/shard_map/conv_values/pallas_call | solution.py:783
  194.7 3.9 %collective-permute-done.12 = bf16[240,384]{1,0:T(8,128)(2,1)S(1)} collective-permute-done((bf16[240,384]{1,0:T(8,128)(2,1)S(1)}, bf16[240,384]{1,0:T(8,128)(2,1)S(1)}, u32[]{:S(2)}, u32[]{:S(2)}) %collective-permute-start.12) | collective-permute-done | bytes 184352 | tf_op jit(solution)/shard_map/ppermute | solution.py:1079
  199.0 9.0 %depth_back.1 = (f32[1024,768]{1,0:T(8,128)S(1)}, bf16[896,384]{1,0:T(8,128)(2,1)S(1)}, bf16[896,384]{1,0:T(8,128)(2,1)S(1)}) custom-call(s32[2]{0:T(128)S(1)} %copy-done.15, bf16[1024,768]{1,0:T(8,128)(2,1)S(1)} %copy-done.10, f32[1024,768]{1,0:T(8,128)S(1)} %copy-done.18, f32[1024,16]{1,0:T(8,128)S(1)} %bitcast.45, f32[9,768]{1,0:T(8,128)S(1)} %copy-done.17, ...), custom_call_target="tpu_custom_call" | custom-call | flops 12000000000 | bytes 10000000 | tf_op jit(solution)/shard_map/depth_back/pallas_call | solution.py:854
  208.1 3.0 collective-permute-start.20
  223.0 4.2 %collective-permute-done.8 = bf16[288,384]{1,0:T(8,128)(2,1)S(1)} collective-permute-done((bf16[288,384]{1,0:T(8,128)(2,1)S(1)}, bf16[288,384]{1,0:T(8,128)(2,1)S(1)}, u32[]{:S(2)}, u32[]{:S(2)}) %collective-permute-start.8) | collective-permute-done | bytes 221216 | tf_op jit(solution)/shard_map/ppermute | solution.py:1079
  229.1 2.8 collective-permute-start.15
  236.9 7.1 %collective-permute-done.18 = bf16[512,768]{1,0:T(8,128)(2,1)S(1)} collective-permute-done((bf16[512,768]{1,0:T(8,128)(2,1)S(1)}, bf16[512,768]{1,0:T(8,128)(2,1)S(1)}, u32[]{:S(2)}, u32[]{:S(2)}) %collective-permute-start.18) | collective-permute-done | bytes 786464 | tf_op jit(solution)/shard_map/ppermute | solution.py:1079
  271.9 3.7 %collective-permute-done.36 = bf16[224,384]{1,0:T(8,128)(2,1)S(1)} collective-permute-done((bf16[224,384]{1,0:T(8,128)(2,1)S(1)}, bf16[224,384]{1,0:T(8,128)(2,1)S(1)}, u32[]{:S(2)}, u32[]{:S(2)}) %collective-permute-start.36) | collective-permute-done | bytes 172064 | tf_op jit(solution)/shard_map/ppermute | solution.py:1079
  275.7 17.0 %collective-permute-done.37 = bf16[224,384]{1,0:T(8,128)(2,1)S(1)} collective-permute-done((bf16[224,384]{1,0:T(8,128)(2,1)S(1)}, bf16[224,384]{1,0:T(8,128)(2,1)S(1)}, u32[]{:S(2)}, u32[]{:S(2)}) %collective-permute-start.37) | collective-permute-done | bytes 172064 | tf_op jit(solution)/shard_map/ppermute | solution.py:1079
  300.5 4.7 %collective-permute-done.40 = bf16[288,384]{1,0:T(8,128)(2,1)S(1)} collective-permute-done((bf16[288,384]{1,0:T(8,128)(2,1)S(1)}, bf16[288,384]{1,0:T(8,128)(2,1)S(1)}, u32[]{:S(2)}, u32[]{:S(2)}) %collective-permute-start.40) | collective-permute-done | bytes 221216 | tf_op jit(solution)/shard_map/ppermute | solution.py:1079
  305.2 4.5 %collective-permute-done.41 = bf16[288,384]{1,0:T(8,128)(2,1)S(1)} collective-permute-done((bf16[288,384]{1,0:T(8,128)(2,1)S(1)}, bf16[288,384]{1,0:T(8,128)(2,1)S(1)}, u32[]{:S(2)}, u32[]{:S(2)}) %collective-permute-start.41) | collective-permute-done | bytes 221216 | tf_op jit(solution)/shard_map/ppermute | solution.py:1079
  320.7 12.1 %unpack_ffn.1 = (f32[3072,384]{1,0:T(8,128)}, f32[2,384,1536]{2,1,0:T(8,128)}, f32[768,768]{1,0:T(8,128)}) custom-call(s32[2]{0:T(128)S(1)} %copy-done.15, bf16[3840,384]{1,0:T(8,128)(2,1)} %pad_maximum_fusion.1.mine_ref, bf16[3840,384]{1,0:T(8,128)(2,1)} %collective-permute-done.44.got_ref), custom_call_target="tpu_custom_call" | custom-call | flops 1000000 | bytes 20000000 | tf_op jit(solution)/shard_map/unpack_ffn/pallas_call | solution.py:1006
  (299 shorter events, 96.7 us)
Async XLA Ops:
  2.8 20.3 %collective-permute-start = (bf16[768,384]{1,0:T(8,128)(2,1)}, bf16[768,384]{1,0:T(8,128)(2,1)}, u32[]{:S(2)}, u32[]{:S(2)}) collective-permute-start(bf16[768,384]{1,0:T(8,128)(2,1)} %dynamic-slice_bitcast_fusion.2), channel_id=1, source_target_pairs={{0,16},{1,17},{2,18},{3,19},{4,20},{5,21},{6,22},{7,23},{8,24},{9,... | collective-permute-start | bytes 1769480 | tf_op jit(solution)/shard_map/ppermute | solution.py:1079
  24.2 35.9 %collective-permute-start.2 = (bf16[512,768]{1,0:T(8,128)(2,1)S(1)}, bf16[512,768]{1,0:T(8,128)(2,1)S(1)}, u32[]{:S(2)}, u32[]{:S(2)}) collective-permute-start(bf16[512,768]{1,0:T(8,128)(2,1)S(1)} %dynamic-slice_bitcast_fusion.1), channel_id=1, source_target_pairs={{0,16},{1,17},{2,18},{3,19},{4,20},{5,21},{6,22},{7,23},{8,24},{9,... | collective-permute-start | bytes 2359304 | tf_op jit(solution)/shard_map/ppermute | solution.py:1079
  117.8 13.9 %collective-permute-start.3 = (bf16[3840,384]{1,0:T(8,128)(2,1)}, bf16[3840,384]{1,0:T(8,128)(2,1)}, u32[]{:S(2)}, u32[]{:S(2)}) collective-permute-start(bf16[3840,384]{1,0:T(8,128)(2,1)} %get-tuple-element.150), channel_id=1, source_target_pairs={{0,1},{1,0},{2,3},{3,2},{4,5},{5,4},{6,7},{7,6},{8,9},{9,8},{10,11... | collective-permute-start | bytes 8847368 | tf_op jit(solution)/shard_map/ppermute | solution.py:1079
  119.7 39.9 %collective-permute-start.5 = (bf16[512,768]{1,0:T(8,128)(2,1)}, bf16[512,768]{1,0:T(8,128)(2,1)S(1)}, u32[]{:S(2)}, u32[]{:S(2)}) collective-permute-start(bf16[512,768]{1,0:T(8,128)(2,1)} %get-tuple-element.167), channel_id=1, source_target_pairs={{0,16},{1,17},{2,18},{3,19},{4,20},{5,21},{6,22},{7,23},{8,24},{9,... | collective-permute-start | bytes 2359304 | tf_op jit(solution)/shard_map/ppermute | solution.py:1079
  134.7 24.6 %collective-permute-start.4 = (bf16[1920,384]{1,0:T(8,128)(2,1)S(1)}, bf16[1920,384]{1,0:T(8,128)(2,1)S(1)}, u32[]{:S(2)}, u32[]{:S(2)}) collective-permute-start(bf16[1920,384]{1,0:T(8,128)(2,1)S(1)} %get-tuple-element.165), channel_id=1, source_target_pairs={{0,2},{1,17},{2,0},{3,19},{4,6},{5,21},{6,4},{7,23},{8,10},{9,25},... | collective-permute-start | bytes 4423688 | tf_op jit(solution)/shard_map/ppermute | solution.py:1079
  159.6 12.5 %collective-permute-start.6 = (bf16[960,384]{1,0:T(8,128)(2,1)S(1)}, bf16[960,384]{1,0:T(8,128)(2,1)S(1)}, u32[]{:S(2)}, u32[]{:S(2)}) collective-permute-start(bf16[960,384]{1,0:T(8,128)(2,1)S(1)} %get-tuple-element.173), channel_id=1, source_target_pairs={{0,16},{1,3},{2,18},{3,1},{4,20},{5,7},{6,22},{7,5},{8,24},{9,11},... | collective-permute-start | bytes 2211848 | tf_op jit(solution)/shard_map/ppermute | solution.py:1079
  178.5 20.1 %collective-permute-start.7 = (bf16[1152,384]{1,0:T(8,128)(2,1)S(1)}, bf16[1152,384]{1,0:T(8,128)(2,1)S(1)}, u32[]{:S(2)}, u32[]{:S(2)}) collective-permute-start(bf16[1152,384]{1,0:T(8,128)(2,1)S(1)} %get-tuple-element.191), channel_id=1, source_target_pairs={{0,1},{1,0},{2,3},{3,2},{4,5},{5,4},{6,7},{7,6},{8,9},{9,8},{10,11... | collective-permute-start | bytes 2654216 | tf_op jit(solution)/shard_map/ppermute | solution.py:1079
  178.6 16.1 %collective-permute-start.13 = (bf16[240,384]{1,0:T(8,128)(2,1)S(1)}, bf16[240,384]{1,0:T(8,128)(2,1)S(1)}, u32[]{:S(2)}, u32[]{:S(2)}) collective-permute-start(bf16[240,384]{1,0:T(8,128)(2,1)S(1)} %get-tuple-element.203), channel_id=1, source_target_pairs={{0,12},{1,13},{2,14},{3,15},{4,8},{5,9},{6,10},{7,11},{8,4},{9,5},... | collective-permute-start | bytes 552968 | tf_op jit(solution)/shard_map/ppermute | solution.py:1079
  182.3 16.2 %collective-permute-start.12 = (bf16[240,384]{1,0:T(8,128)(2,1)S(1)}, bf16[240,384]{1,0:T(8,128)(2,1)S(1)}, u32[]{:S(2)}, u32[]{:S(2)}) collective-permute-start(bf16[240,384]{1,0:T(8,128)(2,1)S(1)} %get-tuple-element.202), channel_id=1, source_target_pairs={{0,8},{1,9},{2,10},{3,11},{4,12},{5,13},{6,14},{7,15},{8,0},{9,1},... | collective-permute-start | bytes 552968 | tf_op jit(solution)/shard_map/ppermute | solution.py:1079
  182.3 16.2 %collective-permute-start.11 = (bf16[240,384]{1,0:T(8,128)(2,1)S(1)}, bf16[240,384]{1,0:T(8,128)(2,1)S(1)}, u32[]{:S(2)}, u32[]{:S(2)}) collective-permute-start(bf16[240,384]{1,0:T(8,128)(2,1)S(1)} %get-tuple-element.201), channel_id=1, source_target_pairs={{0,4},{1,5},{2,6},{3,7},{4,0},{5,1},{6,2},{7,3},{8,12},{9,13},{10,... | collective-permute-start | bytes 552968 | tf_op jit(solution)/shard_map/ppermute | solution.py:1079
  208.1 11.8 %collective-permute-start.20 = (bf16[240,384]{1,0:T(8,128)(2,1)S(1)}, bf16[240,384]{1,0:T(8,128)(2,1)S(1)}, u32[]{:S(2)}, u32[]{:S(2)}) collective-permute-start(bf16[240,384]{1,0:T(8,128)(2,1)S(1)} %add_convert_fusion.8), channel_id=1, source_target_pairs={{0,8},{1,9},{2,10},{3,11},{4,12},{5,13},{6,14},{7,15},{8,0},{9,1},... | collective-permute-start | bytes 552968 | tf_op jit(solution)/shard_map/ppermute | solution.py:1079
  213.6 13.7 %collective-permute-start.14 = (bf16[896,384]{1,0:T(8,128)(2,1)S(1)}, bf16[896,384]{1,0:T(8,128)(2,1)S(1)}, u32[]{:S(2)}, u32[]{:S(2)}) collective-permute-start(bf16[896,384]{1,0:T(8,128)(2,1)S(1)} %get-tuple-element.216), channel_id=1, source_target_pairs={{0,1},{1,0},{2,3},{3,2},{4,5},{5,4},{6,7},{7,6},{8,9},{9,8},{10,11... | collective-permute-start | bytes 2064392 | tf_op jit(solution)/shard_map/ppermute | solution.py:1079
  220.0 24.0 %collective-permute-start.18 = (bf16[512,768]{1,0:T(8,128)(2,1)S(1)}, bf16[512,768]{1,0:T(8,128)(2,1)S(1)}, u32[]{:S(2)}, u32[]{:S(2)}) collective-permute-start(bf16[512,768]{1,0:T(8,128)(2,1)S(1)} %xgrad_far.1), channel_id=1, source_target_pairs={{0,16},{1,17},{2,18},{3,19},{4,20},{5,21},{6,22},{7,23},{8,24},{9,... | collective-permute-start | bytes 2359304 | tf_op jit(solution)/shard_map/ppermute | solution.py:1079
  232.0 18.7 %collective-permute-start.24 = (bf16[224,384]{1,0:T(8,128)(2,1)S(1)}, bf16[224,384]{1,0:T(8,128)(2,1)S(1)}, u32[]{:S(2)}, u32[]{:S(2)}) collective-permute-start(bf16[224,384]{1,0:T(8,128)(2,1)S(1)} %get-tuple-element.234), channel_id=1, source_target_pairs={{0,18},{1,19},{2,16},{3,17},{4,22},{5,23},{6,20},{7,21},{8,26},{9,... | collective-permute-start | bytes 516104 | tf_op jit(solution)/shard_map/ppermute | solution.py:1079
  233.8 16.9 %collective-permute-start.23 = (bf16[224,384]{1,0:T(8,128)(2,1)S(1)}, bf16[224,384]{1,0:T(8,128)(2,1)S(1)}, u32[]{:S(2)}, u32[]{:S(2)}) collective-permute-start(bf16[224,384]{1,0:T(8,128)(2,1)S(1)} %get-tuple-element.233), channel_id=1, source_target_pairs={{0,2},{1,3},{2,0},{3,1},{4,6},{5,7},{6,4},{7,5},{8,10},{9,11},{10,... | collective-permute-start | bytes 516104 | tf_op jit(solution)/shard_map/ppermute | solution.py:1079
  235.8 15.2 %collective-permute-start.22 = (bf16[224,384]{1,0:T(8,128)(2,1)S(1)}, bf16[224,384]{1,0:T(8,128)(2,1)S(1)}, u32[]{:S(2)}, u32[]{:S(2)}) collective-permute-start(bf16[224,384]{1,0:T(8,128)(2,1)S(1)} %get-tuple-element.232), channel_id=1, source_target_pairs={{0,16},{1,17},{2,18},{3,19},{4,20},{5,21},{6,22},{7,23},{8,24},{9,... | collective-permute-start | bytes 516104 | tf_op jit(solution)/shard_map/ppermute | solution.py:1079
  251.1 16.3 %collective-permute-start.25 = (bf16[960,384]{1,0:T(8,128)(2,1)S(1)}, bf16[960,384]{1,0:T(8,128)(2,1)S(1)}, u32[]{:S(2)}, u32[]{:S(2)}) collective-permute-start(bf16[960,384]{1,0:T(8,128)(2,1)S(1)} %constant_dynamic-update-slice_fusion), channel_id=1, source_target_pairs={{0,16},{1,3},{2,18},{3,1},{4,20},{5,7},{6,22},{7,5},{8,24},{9,11},... | collective-permute-start | bytes 2211848 | tf_op jit(solution)/shard_map/ppermute | solution.py:1079
  267.7 25.0 %collective-permute-start.35 = (bf16[1920,384]{1,0:T(8,128)(2,1)S(1)}, bf16[1920,384]{1,0:T(8,128)(2,1)}, u32[]{:S(2)}, u32[]{:S(2)}) collective-permute-start(bf16[1920,384]{1,0:T(8,128)(2,1)S(1)} %pad_maximum_fusion.3), channel_id=1, source_target_pairs={{0,2},{1,17},{2,0},{3,19},{4,6},{5,21},{6,4},{7,23},{8,10},{9,25},... | collective-permute-start | bytes 4423688 | tf_op jit(solution)/shard_map/ppermute | solution.py:1079
  269.3 23.4 %collective-permute-start.37 = (bf16[224,384]{1,0:T(8,128)(2,1)S(1)}, bf16[224,384]{1,0:T(8,128)(2,1)S(1)}, u32[]{:S(2)}, u32[]{:S(2)}) collective-permute-start(bf16[224,384]{1,0:T(8,128)(2,1)S(1)} %constant_dynamic-update-slice_fusion.18), channel_id=1, source_target_pairs={{0,2},{1,3},{2,0},{3,1},{4,6},{5,7},{6,4},{7,5},{8,10},{9,11},{10,... | collective-permute-start | bytes 516104 | tf_op jit(solution)/shard_map/ppermute | solution.py:1079
  270.8 21.9 %collective-permute-start.38 = (bf16[224,384]{1,0:T(8,128)(2,1)S(1)}, bf16[224,384]{1,0:T(8,128)(2,1)S(1)}, u32[]{:S(2)}, u32[]{:S(2)}) collective-permute-start(bf16[224,384]{1,0:T(8,128)(2,1)S(1)} %constant_dynamic-update-slice_fusion.18), channel_id=1, source_target_pairs={{0,18},{1,19},{2,16},{3,17},{4,22},{5,23},{6,20},{7,21},{8,26},{9,... | collective-permute-start | bytes 516104 | tf_op jit(solution)/shard_map/ppermute | solution.py:1079
  296.3 24.4 %collective-permute-start.44 = (bf16[3840,384]{1,0:T(8,128)(2,1)}, bf16[3840,384]{1,0:T(8,128)(2,1)}, u32[]{:S(2)}, u32[]{:S(2)}) collective-permute-start(bf16[3840,384]{1,0:T(8,128)(2,1)} %pad_maximum_fusion.1.mine_ref), channel_id=1, source_target_pairs={{0,1},{1,0},{2,3},{3,2},{4,5},{5,4},{6,7},{7,6},{8,9},{9,8},{10,11... | collective-permute-start | bytes 8847368 | tf_op jit(solution)/shard_map/ppermute | solution.py:1079
  296.3 13.5 %collective-permute-start.39 = (bf16[896,384]{1,0:T(8,128)(2,1)S(1)}, bf16[896,384]{1,0:T(8,128)(2,1)S(1)}, u32[]{:S(2)}, u32[]{:S(2)}) collective-permute-start(bf16[896,384]{1,0:T(8,128)(2,1)S(1)} %constant_dynamic-update-slice_fusion.14.cm_ref), channel_id=1, source_target_pairs={{0,1},{1,0},{2,3},{3,2},{4,5},{5,4},{6,7},{7,6},{8,9},{9,8},{10,11... | collective-permute-start | bytes 2064392 | tf_op jit(solution)/shard_map/ppermute | solution.py:1079
  297.8 11.8 %collective-permute-start.41 = (bf16[288,384]{1,0:T(8,128)(2,1)S(1)}, bf16[288,384]{1,0:T(8,128)(2,1)S(1)}, u32[]{:S(2)}, u32[]{:S(2)}) collective-permute-start(bf16[288,384]{1,0:T(8,128)(2,1)S(1)} %constant_dynamic-update-slice_fusion.7), channel_id=1, source_target_pairs={{0,2},{1,3},{2,0},{3,1},{4,6},{5,7},{6,4},{7,5},{8,10},{9,11},{10,... | collective-permute-start | bytes 663560 | tf_op jit(solution)/shard_map/ppermute | solution.py:1079
  298.3 11.4 %collective-permute-start.42 = (bf16[288,384]{1,0:T(8,128)(2,1)S(1)}, bf16[288,384]{1,0:T(8,128)(2,1)S(1)}, u32[]{:S(2)}, u32[]{:S(2)}) collective-permute-start(bf16[288,384]{1,0:T(8,128)(2,1)S(1)} %constant_dynamic-update-slice_fusion.7), channel_id=1, source_target_pairs={{0,18},{1,19},{2,16},{3,17},{4,22},{5,23},{6,20},{7,21},{8,26},{9,... | collective-permute-start | bytes 663560 | tf_op jit(solution)/shard_map/ppermute | solution.py:1079
  (82 other events, 818.8 us)
